TPU v7x, 32 devices: a whole 2x2x4 slice. The times are simulated.
32 devices in a mesh: mom: 8 (over z, x), tm: 4 (over y, core).
Axes of the slice: x: 2, y: 2, z: 4, core: 2. Of those that a mesh axis runs over, the one named last changes fastest.
Arguments:
- source: float32 [2, 8, 1024, 512], P(None, 'mom', 'tm'), may hold values from -6 to 6
- inverse_diag: float32 [2, 8, 4, 256, 256], P(None, 'mom', 'tm'), may hold values from -0.25 to 0.25
- coupling: float32 [2, 8, 4, 256, 256], P(None, 'mom', 'tm'), may hold values from -0.21875 to 0.21875
- pair_moms: int32 [8, 8, 3], replicated, may hold values from 0 to 7, as said below
- pair_count: int32 [8], replicated, may hold values from 1 to 8
- pair_weight: int32 [8, 8], replicated, may hold values from 0 to 15
- vertex: float32 [16], replicated, may hold values from 0.02 to 0.2
Outputs:
- solved: bfloat16 [2, 8, 1024, 512], P(None, 'mom', 'tm')
- sigma: float32 [2, 8, 1024, 512], P(None, 'mom', 'tm')
Inputs may be any that keep to these rules, and one draw needn't show every extreme that they name: `pair_moms`: entry (k, s) is ((k - q) mod 8, p, (p + q) mod 8) for some q and p.
All inputs are finite; a program needn't handle non-finite values.
Results may differ from a plain program's by a relative error of at most 0.0059.
Values may be sent and summed in bfloat16 or wider, within the bound.
No kernel may reach another device: no remote copies, remote signals or barrier semaphores. Data moves between devices by JAX's collectives and lax.ppermute only.
A program may use at most 64 MiB of HBM per device.

v0:
```python
import functools

import jax
import jax.numpy as jnp
from jax import lax
from jax.experimental import pallas as pl
from jax.experimental.pallas import tpu as pltpu
from jax.sharding import PartitionSpec as P


F32 = jnp.float32
BF16 = jnp.bfloat16
CHUNKS = 2
MIB = 1 << 20


def params(mib):
    return pltpu.CompilerParams(vmem_limit_bytes=mib * MIB)


def cost(flops, moved):
    return pl.CostEstimate(flops=flops, bytes_accessed=moved, transcendentals=0)


def split(value):
    high = value.astype(BF16)
    return high, (value - high.astype(F32)).astype(BF16)


def embed(real, imag):
    return jnp.concatenate(
        [jnp.concatenate([real, -imag], 1), jnp.concatenate([imag, real], 1)], 0
    )


def dot(left, right):
    return lax.dot_general(left, right, (((1,), (0,)), ((), ())), preferred_element_type=F32)


def dot_split(left_high, left_low, right_high, right_low):
    return dot(left_high, right_high) + (dot(left_high, right_low) + dot(left_low, right_high))


def drive_kernel(inverse_ref, source_ref, *refs):
    count = len(refs) - 3
    out_refs = refs[:count]
    inverse, source, sems = refs[count:]
    size = inverse.shape[-1]
    width = out_refs[0].shape[-1]
    copies = [
        pltpu.make_async_copy(inverse_ref.at[part, 0, 0], inverse.at[part], sems.at[part])
        for part in range(2)
    ]
    for chunk in range(count):
        columns = pl.ds(chunk * width, width)
        for part in range(2):
            copies.append(
                pltpu.make_async_copy(
                    source_ref.at[part, 0, :, columns],
                    source.at[pl.ds(part * size, size), columns],
                    sems.at[len(copies)],
                )
            )
    for copy in copies:
        copy.start()
    copies[0].wait()
    copies[1].wait()
    high, low = split(embed(inverse[0], inverse[1]))
    for chunk, out_ref in enumerate(out_refs):
        copies[2 + 2 * chunk].wait()
        copies[3 + 2 * chunk].wait()
        stacked = source[:, chunk * width : (chunk + 1) * width]
        result = dot_split(high, low, *split(stacked))
        out_ref[0] = result[:size]
        out_ref[1] = result[size:]


def propagator_kernel(inverse_ref, coupling_ref, out_ref):
    size = inverse_ref.shape[-1]
    left = split(embed(inverse_ref[0, 0, 0], inverse_ref[1, 0, 0]))
    stacked = jnp.concatenate([coupling_ref[0, 0, 0], coupling_ref[1, 0, 0]], 0)
    result = dot_split(*left, *split(stacked))
    for part in range(2):
        high, low = split(result[part * size : (part + 1) * size])
        out_ref[0, part] = high
        out_ref[1, part] = low


def advance(matrix_ref, incoming_ref):
    high = embed(matrix_ref[0, 0], matrix_ref[0, 1])
    low = embed(matrix_ref[1, 0], matrix_ref[1, 1])
    stacked = jnp.concatenate([incoming_ref[0], incoming_ref[1]], 0)
    if stacked.dtype == BF16:
        return dot(high, stacked) + dot(low, stacked)
    return dot_split(high, low, *split(stacked))


def hop_kernel(matrix_ref, state_ref, incoming_ref, *out_refs):
    size = state_ref.shape[1]
    result = advance(matrix_ref, incoming_ref)
    for part in range(2):
        value = state_ref[part] + result[part * size : (part + 1) * size]
        for out_ref in out_refs:
            out_ref[part] = value.astype(out_ref.dtype)


def last_kernel(order, me_ref, matrix_ref, state_ref, incoming_ref, *refs):
    ready_refs = refs[: CHUNKS - 1]
    solved_ref = refs[CHUNKS - 1]
    piece_refs = refs[CHUNKS:-1]
    hold_ref = refs[-1]
    size, width = state_ref.shape[1:]
    result = advance(matrix_ref, incoming_ref)
    for part in range(2):
        hold_ref[part] = state_ref[part] + result[part * size : (part + 1) * size]
    rows = piece_refs[0].shape[1]
    for chunk, ref in enumerate([*ready_refs, hold_ref]):
        columns = slice(chunk * width, (chunk + 1) * width)
        for step, piece_ref in zip(order, piece_refs):
            owner = jnp.bitwise_xor(me_ref[0], step)
            start = pl.multiple_of(owner * rows, rows)
            for part in range(2):
                piece_ref[part, :, columns] = ref[part, pl.ds(start, rows), :].astype(BF16)
        for part in range(2):
            solved_ref[part, 0, :, columns] = ref[part].astype(BF16)


def energy_kernel(order, targets, me_ref, triples_ref, counts_ref, weights_ref, vertex_ref, *refs):
    count = len(order)
    piece_refs = refs[:count]
    out_refs = refs[count:-1]
    hold_ref = refs[-1]
    slots = weights_ref.shape[1]
    rows, columns = piece_refs[0].shape[1:]
    for step, piece_ref in zip(order, piece_refs):
        owner = jnp.bitwise_xor(me_ref[0], step)
        hold_ref[owner] = piece_ref[...].astype(F32)
    tile = min(rows, 16)
    for step, out_ref in zip(targets, out_refs):
        mom = jnp.bitwise_xor(me_ref[0], step)
        live = jnp.minimum(counts_ref[mom], slots)
        for at in range(0, rows, tile):
            here = pl.ds(at, tile)

            def slot_step(slot, total):
                total_re, total_im = total
                first = triples_ref[mom, 3 * slot]
                second = triples_ref[mom, 3 * slot + 1]
                third = triples_ref[mom, 3 * slot + 2]
                factor = vertex_ref[weights_ref[mom, slot]]
                first_re = hold_ref[first, 0, here, :]
                first_im = hold_ref[first, 1, here, :]
                second_re = hold_ref[second, 0, here, :]
                second_im = hold_ref[second, 1, here, :]
                third_re = hold_ref[third, 0, here, :]
                third_im = hold_ref[third, 1, here, :]
                prod_re = first_re * second_re - first_im * second_im
                prod_im = first_re * second_im + first_im * second_re
                term_re = prod_re * third_re + prod_im * third_im
                term_im = prod_im * third_re - prod_re * third_im
                return total_re + factor * term_re, total_im + factor * term_im

            zero = jnp.zeros((tile, columns), F32)
            total_re, total_im = lax.fori_loop(0, live, slot_step, (zero, zero))
            out_ref[0, here, :] = total_re.astype(BF16)
            out_ref[1, here, :] = total_im.astype(BF16)


def gather_kernel(order, me_ref, *refs):
    piece_refs = refs[:-1]
    out_ref = refs[-1]
    rows = piece_refs[0].shape[1]
    for step, piece_ref in zip(order, piece_refs):
        owner = jnp.bitwise_xor(me_ref[0], step)
        start = pl.multiple_of(owner * rows, rows)
        for part in range(2):
            out_ref[part, 0, pl.ds(start, rows), :] = piece_ref[part].astype(F32)


def step_order(moms):
    return sorted(range(1, moms), key=lambda step: (-step.bit_length(), step))


def local(source, inverse_diag, coupling, pair_moms, pair_count, pair_weight, vertex):
    size = inverse_diag.shape[3]
    columns = source.shape[3]
    width = columns // CHUNKS
    moms = lax.axis_size("mom")
    times = lax.axis_size("tm")
    rows = size // moms
    me = lax.axis_index("mom").astype(jnp.int32).reshape(1)
    order = step_order(moms)
    smem = pl.BlockSpec(memory_space=pltpu.SMEM)
    vmem = pl.BlockSpec(memory_space=pltpu.VMEM)

    drive = pl.pallas_call(
        drive_kernel,
        out_shape=[jax.ShapeDtypeStruct((2, size, width), F32)] * CHUNKS,
        in_specs=[pl.BlockSpec(memory_space=pltpu.HBM)] * 2,
        out_specs=[vmem] * CHUNKS,
        scratch_shapes=[
            pltpu.VMEM((2, size, size), F32),
            pltpu.VMEM((2 * size, columns), F32),
            pltpu.SemaphoreType.DMA((2 + 2 * CHUNKS,)),
        ],
        compiler_params=params(16),
        cost_estimate=cost(24 * size * size * columns, 4 * 4 * size * columns),
        name="drive",
    )(*(pltpu.with_memory_space_constraint(value, pltpu.HBM) for value in (inverse_diag, source)))
    matrix = pl.pallas_call(
        propagator_kernel,
        out_shape=jax.ShapeDtypeStruct((2, 2, size, size), BF16),
        in_specs=[vmem] * 2,
        out_specs=vmem,
        compiler_params=params(16),
        cost_estimate=cost(24 * size**3, 8 * 4 * size * size),
        name="propagator",
    )(inverse_diag, coupling)

    def hop(state, incoming, dtypes):
        return pl.pallas_call(
            hop_kernel,
            out_shape=[jax.ShapeDtypeStruct((2, size, width), dtype) for dtype in dtypes],
            in_specs=[vmem] * 3,
            out_specs=[vmem] * len(dtypes),
            compiler_params=params(16),
            cost_estimate=cost(24 * size * size * width, 8 * 4 * size * width),
            name="hop",
        )(matrix, state, incoming)

    state = list(drive)
    sent = list(drive)
    arrived = [None] * CHUNKS
    for turn in range(times - 1):
        for chunk in range(CHUNKS):
            if turn:
                kinds = [F32] if turn % 2 == 0 else [F32, BF16]
                outs = hop(state[chunk], arrived[chunk], kinds)
                state[chunk], sent[chunk] = outs[0], outs[-1]
            arrived[chunk] = lax.ppermute(sent[chunk], "tm", [(turn, turn + 1)])

    ready = [hop(state[chunk], arrived[chunk], [F32])[0] for chunk in range(CHUNKS - 1)]
    everyone = [*order, 0]
    piece = jax.ShapeDtypeStruct((2, rows, columns), BF16)
    solved, *pieces = pl.pallas_call(
        functools.partial(last_kernel, everyone),
        out_shape=[jax.ShapeDtypeStruct((2, 1, size, columns), BF16)] + [piece] * moms,
        in_specs=[smem] + [vmem] * (2 + CHUNKS),
        out_specs=[vmem] * (1 + moms),
        scratch_shapes=[pltpu.VMEM((2, size, width), F32)],
        compiler_params=params(16),
        cost_estimate=cost(24 * size * size * width, 8 * 4 * size * columns),
        name="last",
    )(me, matrix, state[-1], arrived[-1], *ready)

    def swap(value, step):
        return lax.ppermute(value, "mom", [(at, at ^ step) for at in range(moms)])

    arrived = [swap(value, step) for value, step in zip(pieces, order)] + [pieces[-1]]
    triples = pair_moms.reshape(pair_moms.shape[0], -1)

    def energy(targets):
        return pl.pallas_call(
            functools.partial(energy_kernel, everyone, targets),
            out_shape=[piece] * len(targets),
            in_specs=[smem] * 5 + [vmem] * moms,
            out_specs=[vmem] * len(targets),
            scratch_shapes=[pltpu.VMEM((moms, 2, rows, columns), F32)],
            compiler_params=params(16),
            cost_estimate=cost(100 * rows * columns * 8 * len(targets), 4 * size * columns),
            name="energy",
        )(me, triples, pair_count, pair_weight, vertex, *arrived)

    groups = [everyone[at : at + max(2, moms // 4)] for at in range(0, moms, max(2, moms // 4))]
    home = []
    for targets in groups:
        for step, value in zip(targets, energy(targets)):
            home.append(swap(value, step) if step else value)
    sigma = pl.pallas_call(
        functools.partial(gather_kernel, everyone),
        out_shape=jax.ShapeDtypeStruct((2, 1, size, columns), F32),
        in_specs=[smem] + [vmem] * moms,
        out_specs=vmem,
        compiler_params=params(16),
        cost_estimate=cost(size * columns, 12 * size * columns),
        name="gather",
    )(me, *home)
    return solved, sigma


def solution(mesh):
    return jax.shard_map(
        local,
        mesh=mesh,
        in_specs=(
            P(None, "mom", "tm", None),
            P(None, "mom", "tm", None, None),
            P(None, "mom", "tm", None, None),
            P(),
            P(),
            P(),
            P(),
        ),
        out_specs=(P(None, "mom", "tm", None), P(None, "mom", "tm", None)),
        check_vma=False,
    )
```

profile of v0, /device:TPU:4, one launch (start us, length us, event | category | flops | bytes accessed | tf_op | source)
XLA Modules:
  0.0 63.7 jit_solution(9346187281622054122)
XLA Ops:
  0.6 3.2 %drive.1 = (f32[2,256,256]{2,1,0:T(8,128)S(1)}, f32[2,256,256]{2,1,0:T(8,128)S(1)}) custom-call(f32[2,1,1,256,256]{4,3,2,1,0:T(8,128)} %inverse_ref.3, f32[2,1,256,512]{3,2,1,0:T(8,128)} %source_ref.1), custom_call_target="tpu_custom_call" | custom-call | flops 805306368 | bytes 2097152 | tf_op jit(solution)/shard_map/drive/pallas_call | solution.py:196
  3.9 0.7 %collective-permute-start.3 = (f32[2,256,256]{2,1,0:T(8,128)S(1)}, f32[2,256,256]{2,1,0:T(8,128)S(1)}, u32[]{:S(2)}, u32[]{:S(2)}) collective-permute-start(f32[2,256,256]{2,1,0:T(8,128)S(1)} %get-tuple-element.28.state_ref), channel_id=1, source_target_pairs={{0,1},{4,5},{8,9},{12,13},{16,17},{20,21},{24,25},{28,29}} | collective-permute-start | bytes 1572872 | tf_op jit(solution)/shard_map/ppermute | solution.py:240
  4.6 0.7 %collective-permute-start = (f32[2,256,256]{2,1,0:T(8,128)S(1)}, f32[2,256,256]{2,1,0:T(8,128)S(1)}, u32[]{:S(2)}, u32[]{:S(2)}) collective-permute-start(f32[2,256,256]{2,1,0:T(8,128)S(1)} %get-tuple-element.25.state_ref), channel_id=1, source_target_pairs={{0,1},{4,5},{8,9},{12,13},{16,17},{20,21},{24,25},{28,29}} | collective-permute-start | bytes 1572872 | tf_op jit(solution)/shard_map/ppermute | solution.py:240
  5.3 0.6 propagator.1.matrix_ref
  5.9 0.0 collective-permute-done.3.incoming_ref
  5.9 0.6 hop.7
  6.5 1.3 %collective-permute-start.4 = (bf16[2,256,256]{2,1,0:T(8,128)(2,1)S(1)}, bf16[2,256,256]{2,1,0:T(8,128)(2,1)S(1)}, u32[]{:S(2)}, u32[]{:S(2)}) collective-permute-start(bf16[2,256,256]{2,1,0:T(8,128)(2,1)S(1)} %get-tuple-element.30), channel_id=1, source_target_pairs={{1,2},{5,6},{9,10},{13,14},{17,18},{21,22},{25,26},{29,30}} | collective-permute-start | bytes 786440 | tf_op jit(solution)/shard_map/ppermute | solution.py:240
  7.8 0.6 hop.5
  8.4 1.3 %collective-permute-start.1 = (bf16[2,256,256]{2,1,0:T(8,128)(2,1)S(1)}, bf16[2,256,256]{2,1,0:T(8,128)(2,1)S(1)}, u32[]{:S(2)}, u32[]{:S(2)}) collective-permute-start(bf16[2,256,256]{2,1,0:T(8,128)(2,1)S(1)} %get-tuple-element.27), channel_id=1, source_target_pairs={{1,2},{5,6},{9,10},{13,14},{17,18},{21,22},{25,26},{29,30}} | collective-permute-start | bytes 786440 | tf_op jit(solution)/shard_map/ppermute | solution.py:240
  9.7 4.5 %collective-permute-done.4.incoming_ref = bf16[2,256,256]{2,1,0:T(8,128)(2,1)S(1)} collective-permute-done((bf16[2,256,256]{2,1,0:T(8,128)(2,1)S(1)}, bf16[2,256,256]{2,1,0:T(8,128)(2,1)S(1)}, u32[]{:S(2)}, u32[]{:S(2)}) %collective-permute-start.4) | collective-permute-done | bytes 262176 | tf_op jit(solution)/shard_map/ppermute | solution.py:240
  14.2 0.4 hop.8.state_ref
  14.7 1.3 %collective-permute-start.5 = (f32[2,256,256]{2,1,0:T(8,128)S(1)}, f32[2,256,256]{2,1,0:T(8,128)S(1)}, u32[]{:S(2)}, u32[]{:S(2)}) collective-permute-start(f32[2,256,256]{2,1,0:T(8,128)S(1)} %hop.8.state_ref), channel_id=1, source_target_pairs={{2,3},{6,7},{10,11},{14,15},{18,19},{22,23},{26,27},{30,31}} | collective-permute-start | bytes 1572872 | tf_op jit(solution)/shard_map/ppermute | solution.py:240
  16.0 1.0 %collective-permute-done.1.incoming_ref = bf16[2,256,256]{2,1,0:T(8,128)(2,1)S(1)} collective-permute-done((bf16[2,256,256]{2,1,0:T(8,128)(2,1)S(1)}, bf16[2,256,256]{2,1,0:T(8,128)(2,1)S(1)}, u32[]{:S(2)}, u32[]{:S(2)}) %collective-permute-start.1) | collective-permute-done | bytes 262176 | tf_op jit(solution)/shard_map/ppermute | solution.py:240
  17.0 0.4 hop.6.state_ref
  17.5 1.3 %collective-permute-start.2 = (f32[2,256,256]{2,1,0:T(8,128)S(1)}, f32[2,256,256]{2,1,0:T(8,128)S(1)}, u32[]{:S(2)}, u32[]{:S(2)}) collective-permute-start(f32[2,256,256]{2,1,0:T(8,128)S(1)} %hop.6.state_ref), channel_id=1, source_target_pairs={{2,3},{6,7},{10,11},{14,15},{18,19},{22,23},{26,27},{30,31}} | collective-permute-start | bytes 1572872 | tf_op jit(solution)/shard_map/ppermute | solution.py:240
  18.8 0.6 hop.9.refs_0_
  19.4 0.9 %collective-permute-done.2.incoming_ref = f32[2,256,256]{2,1,0:T(8,128)S(1)} collective-permute-done((f32[2,256,256]{2,1,0:T(8,128)S(1)}, f32[2,256,256]{2,1,0:T(8,128)S(1)}, u32[]{:S(2)}, u32[]{:S(2)}) %collective-permute-start.2) | collective-permute-done | bytes 524320 | tf_op jit(solution)/shard_map/ppermute | solution.py:240
  20.3 1.4 %last.1 = (bf16[2,1,256,512]{3,2,1,0:T(8,128)(2,1)}, bf16[2,32,512]{2,1,0:T(8,128)(2,1)S(1)}, bf16[2,32,512]{2,1,0:T(8,128)(2,1)S(1)}, bf16[2,32,512]{2,1,0:T(8,...) custom-call(s32[1]{0:T(128)} %bitcast.me_ref, ...), custom_call_target="tpu_custom_call" | custom-call | flops 402653184 | bytes 4194304 | tf_op jit(solution)/shard_map/last/pallas_call | solution.py:245
  21.7 1.6 %collective-permute-start.10 = (bf16[2,32,512]{2,1,0:T(8,128)(2,1)S(1)}, bf16[2,32,512]{2,1,0:T(8,128)(2,1)S(1)}, u32[]{:S(2)}, u32[]{:S(2)}) collective-permute-start(bf16[2,32,512]{2,1,0:T(8,128)(2,1)S(1)} %get-tuple-element.36), channel_id=1, source_target_pairs={{0,8},{4,12},{8,0},{12,4},{16,24},{20,28},{24,16},{28,20},{1,9},{5... | collective-permute-start | bytes 196616 | tf_op jit(solution)/shard_map/ppermute | solution.py:257
  23.3 1.4 %collective-permute-start.11 = (bf16[2,32,512]{2,1,0:T(8,128)(2,1)S(1)}, bf16[2,32,512]{2,1,0:T(8,128)(2,1)S(1)}, u32[]{:S(2)}, u32[]{:S(2)}) collective-permute-start(bf16[2,32,512]{2,1,0:T(8,128)(2,1)S(1)} %get-tuple-element.37), channel_id=1, source_target_pairs={{0,12},{4,8},{8,4},{12,0},{16,28},{20,24},{24,20},{28,16},{1,13},{... | collective-permute-start | bytes 196616 | tf_op jit(solution)/shard_map/ppermute | solution.py:257
  24.7 0.5 collective-permute-start.12
  25.2 2.6 %collective-permute-start.6 = (bf16[2,32,512]{2,1,0:T(8,128)(2,1)S(1)}, bf16[2,32,512]{2,1,0:T(8,128)(2,1)S(1)}, u32[]{:S(2)}, u32[]{:S(2)}) collective-permute-start(bf16[2,32,512]{2,1,0:T(8,128)(2,1)S(1)} %get-tuple-element.32), channel_id=1, source_target_pairs={{0,16},{4,20},{8,24},{12,28},{16,0},{20,4},{24,8},{28,12},{1,17},{... | collective-permute-start | bytes 196616 | tf_op jit(solution)/shard_map/ppermute | solution.py:257
  27.8 1.3 %collective-permute-start.7 = (bf16[2,32,512]{2,1,0:T(8,128)(2,1)S(1)}, bf16[2,32,512]{2,1,0:T(8,128)(2,1)S(1)}, u32[]{:S(2)}, u32[]{:S(2)}) collective-permute-start(bf16[2,32,512]{2,1,0:T(8,128)(2,1)S(1)} %get-tuple-element.33), channel_id=1, source_target_pairs={{0,20},{4,16},{8,28},{12,24},{16,4},{20,0},{24,12},{28,8},{1,21},{... | collective-permute-start | bytes 196616 | tf_op jit(solution)/shard_map/ppermute | solution.py:257
  29.1 3.6 %collective-permute-start.8 = (bf16[2,32,512]{2,1,0:T(8,128)(2,1)S(1)}, bf16[2,32,512]{2,1,0:T(8,128)(2,1)S(1)}, u32[]{:S(2)}, u32[]{:S(2)}) collective-permute-start(bf16[2,32,512]{2,1,0:T(8,128)(2,1)S(1)} %get-tuple-element.34), channel_id=1, source_target_pairs={{0,24},{4,28},{8,16},{12,20},{16,8},{20,12},{24,0},{28,4},{1,25},{... | collective-permute-start | bytes 196616 | tf_op jit(solution)/shard_map/ppermute | solution.py:257
  32.7 0.0 collective-permute-done.11.refs_5_
  32.7 0.2 collective-permute-start.9
  32.9 0.1 copy.10
  32.9 0.0 copy-start.2
  33.0 0.1 copy.11.triples_ref
  33.0 0.0 collective-permute-done.12.refs_6_
  33.0 0.0 collective-permute-done.6.refs_0_
  33.0 4.7 %collective-permute-done.7.refs_1_ = bf16[2,32,512]{2,1,0:T(8,128)(2,1)S(1)} collective-permute-done((bf16[2,32,512]{2,1,0:T(8,128)(2,1)S(1)}, bf16[2,32,512]{2,1,0:T(8,128)(2,1)S(1)}, u32[]{:S(2)}, u32[]{:S(2)}) %collective-permute-start.7) | collective-permute-done | bytes 65568 | tf_op jit(solution)/shard_map/ppermute | solution.py:257
  37.7 2.0 %collective-permute-done.9.refs_3_ = bf16[2,32,512]{2,1,0:T(8,128)(2,1)S(1)} collective-permute-done((bf16[2,32,512]{2,1,0:T(8,128)(2,1)S(1)}, bf16[2,32,512]{2,1,0:T(8,128)(2,1)S(1)}, u32[]{:S(2)}, u32[]{:S(2)}) %collective-permute-start.9) | collective-permute-done | bytes 65568 | tf_op jit(solution)/shard_map/ppermute | solution.py:257
  39.7 1.3 %energy.7 = (bf16[2,32,512]{2,1,0:T(8,128)(2,1)S(1)}, bf16[2,32,512]{2,1,0:T(8,128)(2,1)S(1)}) custom-call(s32[1]{0:T(128)} %bitcast.me_ref, s32[8,24]{1,0:T(8,128)S(1)} %copy.11.triples_ref, s32[8]{0:T(128)S(1)} %copy-done.3, s32[8,8]{1,0:T(8,128)S(1)} %copy-done.2, f32[16]{0:T(128)S(1)} %copy-done.4, ...), custom_call_target="tpu_custom_call" | custom-call | flops 26214400 | bytes 524288 | tf_op jit(solution)/shard_map/energy/pallas_call | solution.py:263
  41.1 0.6 collective-permute-start.19
  41.7 1.3 %energy.6 = (bf16[2,32,512]{2,1,0:T(8,128)(2,1)S(1)}, bf16[2,32,512]{2,1,0:T(8,128)(2,1)S(1)}) custom-call(s32[1]{0:T(128)} %bitcast.me_ref, s32[8,24]{1,0:T(8,128)S(1)} %copy.11.triples_ref, s32[8]{0:T(128)S(1)} %copy-done.3, s32[8,8]{1,0:T(8,128)S(1)} %copy-done.2, f32[16]{0:T(128)S(1)} %copy-done.4, ...), custom_call_target="tpu_custom_call" | custom-call | flops 26214400 | bytes 524288 | tf_op jit(solution)/shard_map/energy/pallas_call | solution.py:263
  43.0 2.0 %collective-permute-start.17 = (bf16[2,32,512]{2,1,0:T(8,128)(2,1)S(1)}, bf16[2,32,512]{2,1,0:T(8,128)(2,1)S(1)}, u32[]{:S(2)}, u32[]{:S(2)}) collective-permute-start(bf16[2,32,512]{2,1,0:T(8,128)(2,1)S(1)} %get-tuple-element.44), channel_id=1, source_target_pairs={{0,8},{4,12},{8,0},{12,4},{16,24},{20,28},{24,16},{28,20},{1,9},{5... | collective-permute-start | bytes 196616 | tf_op jit(solution)/shard_map/ppermute | solution.py:257
  45.0 1.0 %collective-permute-start.18 = (bf16[2,32,512]{2,1,0:T(8,128)(2,1)S(1)}, bf16[2,32,512]{2,1,0:T(8,128)(2,1)S(1)}, u32[]{:S(2)}, u32[]{:S(2)}) collective-permute-start(bf16[2,32,512]{2,1,0:T(8,128)(2,1)S(1)} %get-tuple-element.45), channel_id=1, source_target_pairs={{0,12},{4,8},{8,4},{12,0},{16,28},{20,24},{24,20},{28,16},{1,13},{... | collective-permute-start | bytes 196616 | tf_op jit(solution)/shard_map/ppermute | solution.py:257
  46.0 1.6 %energy.5 = (bf16[2,32,512]{2,1,0:T(8,128)(2,1)S(1)}, bf16[2,32,512]{2,1,0:T(8,128)(2,1)S(1)}) custom-call(s32[1]{0:T(128)} %bitcast.me_ref, s32[8,24]{1,0:T(8,128)S(1)} %copy.11.triples_ref, s32[8]{0:T(128)S(1)} %copy-done.3, s32[8,8]{1,0:T(8,128)S(1)} %copy-done.2, f32[16]{0:T(128)S(1)} %copy-done.4, ...), custom_call_target="tpu_custom_call" | custom-call | flops 26214400 | bytes 524288 | tf_op jit(solution)/shard_map/energy/pallas_call | solution.py:263
  47.7 2.8 %collective-permute-start.15 = (bf16[2,32,512]{2,1,0:T(8,128)(2,1)S(1)}, bf16[2,32,512]{2,1,0:T(8,128)(2,1)S(1)}, u32[]{:S(2)}, u32[]{:S(2)}) collective-permute-start(bf16[2,32,512]{2,1,0:T(8,128)(2,1)S(1)} %get-tuple-element.42), channel_id=1, source_target_pairs={{0,24},{4,28},{8,16},{12,20},{16,8},{20,12},{24,0},{28,4},{1,25},{... | collective-permute-start | bytes 196616 | tf_op jit(solution)/shard_map/ppermute | solution.py:257
  50.4 1.1 %collective-permute-start.16 = (bf16[2,32,512]{2,1,0:T(8,128)(2,1)S(1)}, bf16[2,32,512]{2,1,0:T(8,128)(2,1)S(1)}, u32[]{:S(2)}, u32[]{:S(2)}) collective-permute-start(bf16[2,32,512]{2,1,0:T(8,128)(2,1)S(1)} %get-tuple-element.43), channel_id=1, source_target_pairs={{0,28},{4,24},{8,20},{12,16},{16,12},{20,8},{24,4},{28,0},{1,29},{... | collective-permute-start | bytes 196616 | tf_op jit(solution)/shard_map/ppermute | solution.py:257
  51.5 1.3 %energy.4 = (bf16[2,32,512]{2,1,0:T(8,128)(2,1)S(1)}, bf16[2,32,512]{2,1,0:T(8,128)(2,1)S(1)}) custom-call(s32[1]{0:T(128)} %bitcast.me_ref, s32[8,24]{1,0:T(8,128)S(1)} %copy.11.triples_ref, s32[8]{0:T(128)S(1)} %copy-done.3, s32[8,8]{1,0:T(8,128)S(1)} %copy-done.2, f32[16]{0:T(128)S(1)} %copy-done.4, ...), custom_call_target="tpu_custom_call" | custom-call | flops 26214400 | bytes 524288 | tf_op jit(solution)/shard_map/energy/pallas_call | solution.py:263
  52.8 1.5 %collective-permute-start.13 = (bf16[2,32,512]{2,1,0:T(8,128)(2,1)S(1)}, bf16[2,32,512]{2,1,0:T(8,128)(2,1)S(1)}, u32[]{:S(2)}, u32[]{:S(2)}) collective-permute-start(bf16[2,32,512]{2,1,0:T(8,128)(2,1)S(1)} %get-tuple-element.40), channel_id=1, source_target_pairs={{0,16},{4,20},{8,24},{12,28},{16,0},{20,4},{24,8},{28,12},{1,17},{... | collective-permute-start | bytes 196616 | tf_op jit(solution)/shard_map/ppermute | solution.py:257
  54.3 2.4 %collective-permute-start.14 = (bf16[2,32,512]{2,1,0:T(8,128)(2,1)S(1)}, bf16[2,32,512]{2,1,0:T(8,128)(2,1)S(1)}, u32[]{:S(2)}, u32[]{:S(2)}) collective-permute-start(bf16[2,32,512]{2,1,0:T(8,128)(2,1)S(1)} %get-tuple-element.41), channel_id=1, source_target_pairs={{0,20},{4,16},{8,28},{12,24},{16,4},{20,0},{24,12},{28,8},{1,21},{... | collective-permute-start | bytes 196616 | tf_op jit(solution)/shard_map/ppermute | solution.py:257
  56.7 1.1 %collective-permute-done.16.refs_3_ = bf16[2,32,512]{2,1,0:T(8,128)(2,1)S(1)} collective-permute-done((bf16[2,32,512]{2,1,0:T(8,128)(2,1)S(1)}, bf16[2,32,512]{2,1,0:T(8,128)(2,1)S(1)}, u32[]{:S(2)}, u32[]{:S(2)}) %collective-permute-start.16) | collective-permute-done | bytes 65568 | tf_op jit(solution)/shard_map/ppermute | solution.py:257
  57.8 3.0 %collective-permute-done.13.refs_0_ = bf16[2,32,512]{2,1,0:T(8,128)(2,1)S(1)} collective-permute-done((bf16[2,32,512]{2,1,0:T(8,128)(2,1)S(1)}, bf16[2,32,512]{2,1,0:T(8,128)(2,1)S(1)}, u32[]{:S(2)}, u32[]{:S(2)}) %collective-permute-start.13) | collective-permute-done | bytes 65568 | tf_op jit(solution)/shard_map/ppermute | solution.py:257
  60.8 1.8 %collective-permute-done.14.refs_1_ = bf16[2,32,512]{2,1,0:T(8,128)(2,1)S(1)} collective-permute-done((bf16[2,32,512]{2,1,0:T(8,128)(2,1)S(1)}, bf16[2,32,512]{2,1,0:T(8,128)(2,1)S(1)}, u32[]{:S(2)}, u32[]{:S(2)}) %collective-permute-start.14) | collective-permute-done | bytes 65568 | tf_op jit(solution)/shard_map/ppermute | solution.py:257
  62.6 1.0 %gather.1 = f32[2,1,256,512]{3,2,1,0:T(8,128)} custom-call(s32[1]{0:T(128)} %bitcast.me_ref, bf16[2,32,512]{2,1,0:T(8,128)(2,1)S(1)} %collective-permute-done.13.refs_0_, bf16[2,32,512]{2,1,0:T(8,128)(2,1)S(1)} %collective-permute-done.14.refs_1_, bf16[2,32,512]{2,1,0:T(8,128)(2,1)S(1)} %collective-permute-done.15.refs_2_, ...), custom_call_target="tpu_custom_call" | custom-call | flops 131072 | bytes 1572864 | tf_op jit(solution)/shard_map/gather/pallas_call | solution.py:279
  (20 shorter events, 0.1 us)
Async XLA Ops:
  0.6 4.7 %copy-start = (f32[2,1,1,256,256]{4,3,2,1,0:T(8,128)S(1)}, f32[2,1,1,256,256]{4,3,2,1,0:T(8,128)}, u32[]{:S(2)}) copy-start(f32[2,1,1,256,256]{4,3,2,1,0:T(8,128)} %inverse_ref.3) | copy-start | bytes 1572868
  0.6 4.7 %copy-start.1 = (f32[2,1,1,256,256]{4,3,2,1,0:T(8,128)S(1)}, f32[2,1,1,256,256]{4,3,2,1,0:T(8,128)}, u32[]{:S(2)}) copy-start(f32[2,1,1,256,256]{4,3,2,1,0:T(8,128)} %coupling_ref.1) | copy-start | bytes 1572868
  3.9 2.0 %collective-permute-start.3 = (f32[2,256,256]{2,1,0:T(8,128)S(1)}, f32[2,256,256]{2,1,0:T(8,128)S(1)}, u32[]{:S(2)}, u32[]{:S(2)}) collective-permute-start(f32[2,256,256]{2,1,0:T(8,128)S(1)} %get-tuple-element.28.state_ref), channel_id=1, source_target_pairs={{0,1},{4,5},{8,9},{12,13},{16,17},{20,21},{24,25},{28,29}} | collective-permute-start | bytes 1572872 | tf_op jit(solution)/shard_map/ppermute | solution.py:240
  4.6 3.2 %collective-permute-start = (f32[2,256,256]{2,1,0:T(8,128)S(1)}, f32[2,256,256]{2,1,0:T(8,128)S(1)}, u32[]{:S(2)}, u32[]{:S(2)}) collective-permute-start(f32[2,256,256]{2,1,0:T(8,128)S(1)} %get-tuple-element.25.state_ref), channel_id=1, source_target_pairs={{0,1},{4,5},{8,9},{12,13},{16,17},{20,21},{24,25},{28,29}} | collective-permute-start | bytes 1572872 | tf_op jit(solution)/shard_map/ppermute | solution.py:240
  6.5 7.7 %collective-permute-start.4 = (bf16[2,256,256]{2,1,0:T(8,128)(2,1)S(1)}, bf16[2,256,256]{2,1,0:T(8,128)(2,1)S(1)}, u32[]{:S(2)}, u32[]{:S(2)}) collective-permute-start(bf16[2,256,256]{2,1,0:T(8,128)(2,1)S(1)} %get-tuple-element.30), channel_id=1, source_target_pairs={{1,2},{5,6},{9,10},{13,14},{17,18},{21,22},{25,26},{29,30}} | collective-permute-start | bytes 786440 | tf_op jit(solution)/shard_map/ppermute | solution.py:240
  8.4 8.6 %collective-permute-start.1 = (bf16[2,256,256]{2,1,0:T(8,128)(2,1)S(1)}, bf16[2,256,256]{2,1,0:T(8,128)(2,1)S(1)}, u32[]{:S(2)}, u32[]{:S(2)}) collective-permute-start(bf16[2,256,256]{2,1,0:T(8,128)(2,1)S(1)} %get-tuple-element.27), channel_id=1, source_target_pairs={{1,2},{5,6},{9,10},{13,14},{17,18},{21,22},{25,26},{29,30}} | collective-permute-start | bytes 786440 | tf_op jit(solution)/shard_map/ppermute | solution.py:240
  14.7 4.1 %collective-permute-start.5 = (f32[2,256,256]{2,1,0:T(8,128)S(1)}, f32[2,256,256]{2,1,0:T(8,128)S(1)}, u32[]{:S(2)}, u32[]{:S(2)}) collective-permute-start(f32[2,256,256]{2,1,0:T(8,128)S(1)} %hop.8.state_ref), channel_id=1, source_target_pairs={{2,3},{6,7},{10,11},{14,15},{18,19},{22,23},{26,27},{30,31}} | collective-permute-start | bytes 1572872 | tf_op jit(solution)/shard_map/ppermute | solution.py:240
  17.5 2.8 %collective-permute-start.2 = (f32[2,256,256]{2,1,0:T(8,128)S(1)}, f32[2,256,256]{2,1,0:T(8,128)S(1)}, u32[]{:S(2)}, u32[]{:S(2)}) collective-permute-start(f32[2,256,256]{2,1,0:T(8,128)S(1)} %hop.6.state_ref), channel_id=1, source_target_pairs={{2,3},{6,7},{10,11},{14,15},{18,19},{22,23},{26,27},{30,31}} | collective-permute-start | bytes 1572872 | tf_op jit(solution)/shard_map/ppermute | solution.py:240
  21.7 11.2 %copy-start.5 = (s32[8,8,3]{1,0,2:T(8,128)S(1)}, s32[8,8,3]{1,0,2:T(8,128)}, u32[]{:S(2)}) copy-start(s32[8,8,3]{1,0,2:T(8,128)} %param.10) | copy-start | bytes 2308
  21.7 7.4 %collective-permute-start.10 = (bf16[2,32,512]{2,1,0:T(8,128)(2,1)S(1)}, bf16[2,32,512]{2,1,0:T(8,128)(2,1)S(1)}, u32[]{:S(2)}, u32[]{:S(2)}) collective-permute-start(bf16[2,32,512]{2,1,0:T(8,128)(2,1)S(1)} %get-tuple-element.36), channel_id=1, source_target_pairs={{0,8},{4,12},{8,0},{12,4},{16,24},{20,28},{24,16},{28,20},{1,9},{5... | collective-permute-start | bytes 196616 | tf_op jit(solution)/shard_map/ppermute | solution.py:257
  23.3 9.4 %collective-permute-start.11 = (bf16[2,32,512]{2,1,0:T(8,128)(2,1)S(1)}, bf16[2,32,512]{2,1,0:T(8,128)(2,1)S(1)}, u32[]{:S(2)}, u32[]{:S(2)}) collective-permute-start(bf16[2,32,512]{2,1,0:T(8,128)(2,1)S(1)} %get-tuple-element.37), channel_id=1, source_target_pairs={{0,12},{4,8},{8,4},{12,0},{16,28},{20,24},{24,20},{28,16},{1,13},{... | collective-permute-start | bytes 196616 | tf_op jit(solution)/shard_map/ppermute | solution.py:257
  24.7 8.4 %collective-permute-start.12 = (bf16[2,32,512]{2,1,0:T(8,128)(2,1)S(1)}, bf16[2,32,512]{2,1,0:T(8,128)(2,1)S(1)}, u32[]{:S(2)}, u32[]{:S(2)}) collective-permute-start(bf16[2,32,512]{2,1,0:T(8,128)(2,1)S(1)} %get-tuple-element.38), channel_id=1, source_target_pairs={{0,4},{4,0},{8,12},{12,8},{16,20},{20,16},{24,28},{28,24},{1,5},{5... | collective-permute-start | bytes 196616 | tf_op jit(solution)/shard_map/ppermute | solution.py:257
  25.2 7.8 %collective-permute-start.6 = (bf16[2,32,512]{2,1,0:T(8,128)(2,1)S(1)}, bf16[2,32,512]{2,1,0:T(8,128)(2,1)S(1)}, u32[]{:S(2)}, u32[]{:S(2)}) collective-permute-start(bf16[2,32,512]{2,1,0:T(8,128)(2,1)S(1)} %get-tuple-element.32), channel_id=1, source_target_pairs={{0,16},{4,20},{8,24},{12,28},{16,0},{20,4},{24,8},{28,12},{1,17},{... | collective-permute-start | bytes 196616 | tf_op jit(solution)/shard_map/ppermute | solution.py:257
  27.8 10.0 %collective-permute-start.7 = (bf16[2,32,512]{2,1,0:T(8,128)(2,1)S(1)}, bf16[2,32,512]{2,1,0:T(8,128)(2,1)S(1)}, u32[]{:S(2)}, u32[]{:S(2)}) collective-permute-start(bf16[2,32,512]{2,1,0:T(8,128)(2,1)S(1)} %get-tuple-element.33), channel_id=1, source_target_pairs={{0,20},{4,16},{8,28},{12,24},{16,4},{20,0},{24,12},{28,8},{1,21},{... | collective-permute-start | bytes 196616 | tf_op jit(solution)/shard_map/ppermute | solution.py:257
  29.1 8.7 %collective-permute-start.8 = (bf16[2,32,512]{2,1,0:T(8,128)(2,1)S(1)}, bf16[2,32,512]{2,1,0:T(8,128)(2,1)S(1)}, u32[]{:S(2)}, u32[]{:S(2)}) collective-permute-start(bf16[2,32,512]{2,1,0:T(8,128)(2,1)S(1)} %get-tuple-element.34), channel_id=1, source_target_pairs={{0,24},{4,28},{8,16},{12,20},{16,8},{20,12},{24,0},{28,4},{1,25},{... | collective-permute-start | bytes 196616 | tf_op jit(solution)/shard_map/ppermute | solution.py:257
  32.7 7.1 %collective-permute-start.9 = (bf16[2,32,512]{2,1,0:T(8,128)(2,1)S(1)}, bf16[2,32,512]{2,1,0:T(8,128)(2,1)S(1)}, u32[]{:S(2)}, u32[]{:S(2)}) collective-permute-start(bf16[2,32,512]{2,1,0:T(8,128)(2,1)S(1)} %get-tuple-element.35), channel_id=1, source_target_pairs={{0,28},{4,24},{8,20},{12,16},{16,12},{20,8},{24,4},{28,0},{1,29},{... | collective-permute-start | bytes 196616 | tf_op jit(solution)/shard_map/ppermute | solution.py:257
  32.9 6.8 %copy-start.2 = (s32[8,8]{1,0:T(8,128)S(1)}, s32[8,8]{1,0:T(8,128)}, u32[]{:S(2)}) copy-start(s32[8,8]{1,0:T(8,128)} %weights_ref.7) | copy-start | bytes 772
  33.0 6.7 %copy-start.3 = (s32[8]{0:T(128)S(1)}, s32[8]{0:T(128)}, u32[]{:S(2)}) copy-start(s32[8]{0:T(128)} %counts_ref.7) | copy-start | bytes 100
  33.0 6.7 %copy-start.4 = (f32[16]{0:T(128)S(1)}, f32[16]{0:T(128)}, u32[]{:S(2)}) copy-start(f32[16]{0:T(128)} %vertex_ref.7) | copy-start | bytes 196
  41.1 11.7 %collective-permute-start.19 = (bf16[2,32,512]{2,1,0:T(8,128)(2,1)S(1)}, bf16[2,32,512]{2,1,0:T(8,128)(2,1)S(1)}, u32[]{:S(2)}, u32[]{:S(2)}) collective-permute-start(bf16[2,32,512]{2,1,0:T(8,128)(2,1)S(1)} %get-tuple-element.46), channel_id=1, source_target_pairs={{0,4},{4,0},{8,12},{12,8},{16,20},{20,16},{24,28},{28,24},{1,5},{5... | collective-permute-start | bytes 196616 | tf_op jit(solution)/shard_map/ppermute | solution.py:257
  43.0 11.3 %collective-permute-start.17 = (bf16[2,32,512]{2,1,0:T(8,128)(2,1)S(1)}, bf16[2,32,512]{2,1,0:T(8,128)(2,1)S(1)}, u32[]{:S(2)}, u32[]{:S(2)}) collective-permute-start(bf16[2,32,512]{2,1,0:T(8,128)(2,1)S(1)} %get-tuple-element.44), channel_id=1, source_target_pairs={{0,8},{4,12},{8,0},{12,4},{16,24},{20,28},{24,16},{28,20},{1,9},{5... | collective-permute-start | bytes 196616 | tf_op jit(solution)/shard_map/ppermute | solution.py:257
  45.0 11.7 %collective-permute-start.18 = (bf16[2,32,512]{2,1,0:T(8,128)(2,1)S(1)}, bf16[2,32,512]{2,1,0:T(8,128)(2,1)S(1)}, u32[]{:S(2)}, u32[]{:S(2)}) collective-permute-start(bf16[2,32,512]{2,1,0:T(8,128)(2,1)S(1)} %get-tuple-element.45), channel_id=1, source_target_pairs={{0,12},{4,8},{8,4},{12,0},{16,28},{20,24},{24,20},{28,16},{1,13},{... | collective-permute-start | bytes 196616 | tf_op jit(solution)/shard_map/ppermute | solution.py:257
  47.7 9.1 %collective-permute-start.15 = (bf16[2,32,512]{2,1,0:T(8,128)(2,1)S(1)}, bf16[2,32,512]{2,1,0:T(8,128)(2,1)S(1)}, u32[]{:S(2)}, u32[]{:S(2)}) collective-permute-start(bf16[2,32,512]{2,1,0:T(8,128)(2,1)S(1)} %get-tuple-element.42), channel_id=1, source_target_pairs={{0,24},{4,28},{8,16},{12,20},{16,8},{20,12},{24,0},{28,4},{1,25},{... | collective-permute-start | bytes 196616 | tf_op jit(solution)/shard_map/ppermute | solution.py:257
  50.4 7.4 %collective-permute-start.16 = (bf16[2,32,512]{2,1,0:T(8,128)(2,1)S(1)}, bf16[2,32,512]{2,1,0:T(8,128)(2,1)S(1)}, u32[]{:S(2)}, u32[]{:S(2)}) collective-permute-start(bf16[2,32,512]{2,1,0:T(8,128)(2,1)S(1)} %get-tuple-element.43), channel_id=1, source_target_pairs={{0,28},{4,24},{8,20},{12,16},{16,12},{20,8},{24,4},{28,0},{1,29},{... | collective-permute-start | bytes 196616 | tf_op jit(solution)/shard_map/ppermute | solution.py:257
  52.8 8.0 %collective-permute-start.13 = (bf16[2,32,512]{2,1,0:T(8,128)(2,1)S(1)}, bf16[2,32,512]{2,1,0:T(8,128)(2,1)S(1)}, u32[]{:S(2)}, u32[]{:S(2)}) collective-permute-start(bf16[2,32,512]{2,1,0:T(8,128)(2,1)S(1)} %get-tuple-element.40), channel_id=1, source_target_pairs={{0,16},{4,20},{8,24},{12,28},{16,0},{20,4},{24,8},{28,12},{1,17},{... | collective-permute-start | bytes 196616 | tf_op jit(solution)/shard_map/ppermute | solution.py:257
  54.3 8.3 %collective-permute-start.14 = (bf16[2,32,512]{2,1,0:T(8,128)(2,1)S(1)}, bf16[2,32,512]{2,1,0:T(8,128)(2,1)S(1)}, u32[]{:S(2)}, u32[]{:S(2)}) collective-permute-start(bf16[2,32,512]{2,1,0:T(8,128)(2,1)S(1)} %get-tuple-element.41), channel_id=1, source_target_pairs={{0,20},{4,16},{8,28},{12,24},{16,4},{20,0},{24,12},{28,8},{1,21},{... | collective-permute-start | bytes 196616 | tf_op jit(solution)/shard_map/ppermute | solution.py:257
where the time goes:
time: 63.9 us; the launch traced here: 63.7 us
  starting transfers between devices  29.2 us (46%)
  waiting for transfers between devices  19 us (30%)
  Pallas kernels  14.5 us (23%)
  between operations  0.87 us (1%)
    ppermute x14, starting transfers between devices, swap(): return lax.ppermute(value, 'mom', [(at, at ^ step) for at in range(moms)])  22.5 us
    ppermute x14, waiting for transfers between devices, swap(): return lax.ppermute(value, 'mom', [(at, at ^ step) for at in range(moms)])  12.6 us
    ppermute x6, starting transfers between devices, local(): arrived[chunk] = lax.ppermute(sent[chunk], 'tm', [(turn, turn + 1)])  6.62 us
    ppermute x6, waiting for transfers between devices, local(): arrived[chunk] = lax.ppermute(sent[chunk], 'tm', [(turn, turn + 1)])  6.41 us
    pallas_call x4, Pallas kernels, energy(): pl.pallas_call(functools.partial(energy_kernel, everyone, targets), out_s...  5.54 us
    pallas_call x1, Pallas kernels, local(): pl.pallas_call(drive_kernel, out_shape=[jax.ShapeDtypeStruct((2, size, wi...  3.25 us
    pallas_call x5, Pallas kernels, hop(): pl.pallas_call(hop_kernel, out_shape=[jax.ShapeDtypeStruct((2, size, widt...  2.63 us
    pallas_call x1, Pallas kernels, local(): pl.pallas_call(functools.partial(last_kernel, everyone), out_shape=[jax.S...  1.42 us
  transfers between devices with their start and end apart: 20, of which 8 were waited for; matrix products, arithmetic and copies ran while one was open for 0% of the time, Pallas kernels for 12%

commit v1 on v0

v1 whole, which is shorter than its diff:
```python
import functools

import jax
import jax.numpy as jnp
from jax import lax
from jax.experimental import pallas as pl
from jax.experimental.pallas import tpu as pltpu
from jax.sharding import PartitionSpec as P


F32 = jnp.float32
BF16 = jnp.bfloat16
SHARES = (1, 1)
MIB = 1 << 20


def params(mib):
    return pltpu.CompilerParams(vmem_limit_bytes=mib * MIB)


def cost(flops, moved):
    return pl.CostEstimate(flops=flops, bytes_accessed=moved, transcendentals=0)


def split(value):
    high = value.astype(BF16)
    return high, (value - high.astype(F32)).astype(BF16)


def embed(real, imag):
    return jnp.concatenate(
        [jnp.concatenate([real, -imag], 1), jnp.concatenate([imag, real], 1)], 0
    )


def dot(left, right):
    return lax.dot_general(left, right, (((1,), (0,)), ((), ())), preferred_element_type=F32)


def dot_split(left_high, left_low, right_high, right_low):
    return dot(left_high, right_high) + (dot(left_high, right_low) + dot(left_low, right_high))


def load_kernel(inverse_ref, coupling_ref, source_ref, out_ref, inverse, coupling, *rest):
    *later, source, sems = rest
    size, _ = out_ref.shape[1:]
    moves = [(inverse_ref.at[:, 0, 0], inverse)]
    start = 0
    for target in [source, *later]:
        span = target.shape[-1]
        moves.append((source_ref.at[:, 0, :, pl.ds(start, span)], target))
        start += span
    moves.append((coupling_ref.at[:, 0, 0], coupling))
    copies = [
        pltpu.make_async_copy(origin, target, sems.at[at])
        for at, (origin, target) in enumerate(moves)
    ]
    for copy in copies:
        copy.start()
    copies[0].wait()
    high, low = split(embed(inverse[0], inverse[1]))
    copies[1].wait()
    stacked = jnp.concatenate([source[0], source[1]], 0)
    result = dot_split(high, low, *split(stacked))
    out_ref[0] = result[:size]
    out_ref[1] = result[size:]
    for copy in copies[2:]:
        copy.wait()


def drive_kernel(inverse_ref, source_ref, out_ref):
    size = inverse_ref.shape[-1]
    left = split(embed(inverse_ref[0], inverse_ref[1]))
    stacked = jnp.concatenate([source_ref[0], source_ref[1]], 0)
    result = dot_split(*left, *split(stacked))
    out_ref[0] = result[:size]
    out_ref[1] = result[size:]


def propagator_kernel(inverse_ref, coupling_ref, out_ref):
    size = inverse_ref.shape[-1]
    left = split(embed(inverse_ref[0], inverse_ref[1]))
    stacked = jnp.concatenate([coupling_ref[0], coupling_ref[1]], 0)
    result = dot_split(*left, *split(stacked))
    for part in range(2):
        high, low = split(result[part * size : (part + 1) * size])
        out_ref[0, part] = high
        out_ref[1, part] = low


def advance(matrix_ref, incoming_ref):
    high = embed(matrix_ref[0, 0], matrix_ref[0, 1])
    low = embed(matrix_ref[1, 0], matrix_ref[1, 1])
    stacked = jnp.concatenate([incoming_ref[0], incoming_ref[1]], 0)
    if stacked.dtype == BF16:
        return dot(high, stacked) + dot(low, stacked)
    return dot_split(high, low, *split(stacked))


def hop_kernel(matrix_ref, state_ref, incoming_ref, *out_refs):
    size = state_ref.shape[1]
    result = advance(matrix_ref, incoming_ref)
    for part in range(2):
        value = state_ref[part] + result[part * size : (part + 1) * size]
        for out_ref in out_refs:
            out_ref[part] = value.astype(out_ref.dtype)


def last_kernel(order, me_ref, matrix_ref, state_ref, incoming_ref, *refs):
    chunks = len(refs) - len(order)
    ready_refs = refs[: chunks - 1]
    piece_refs = refs[chunks - 1 : -1]
    hold_ref = refs[-1]
    size, _ = state_ref.shape[1:]
    result = advance(matrix_ref, incoming_ref)
    for part in range(2):
        hold_ref[part] = state_ref[part] + result[part * size : (part + 1) * size]
    rows = piece_refs[0].shape[1]
    first = 0
    for ref in [*ready_refs, hold_ref]:
        columns = slice(first, first + ref.shape[-1])
        first += ref.shape[-1]
        for step, piece_ref in zip(order, piece_refs):
            owner = jnp.bitwise_xor(me_ref[0], step)
            start = pl.multiple_of(owner * rows, rows)
            for part in range(2):
                piece_ref[part, :, columns] = ref[part, pl.ds(start, rows), :].astype(BF16)


def emit_kernel(*refs):
    *ready_refs, solved_ref = refs
    first = 0
    for ref in ready_refs:
        columns = slice(first, first + ref.shape[-1])
        first += ref.shape[-1]
        for part in range(2):
            solved_ref[part, 0, :, columns] = ref[part].astype(BF16)


def energy_kernel(order, targets, me_ref, triples_ref, counts_ref, weights_ref, vertex_ref, *refs):
    count = len(order)
    piece_refs = refs[:count]
    out_refs = refs[count:-2]
    hold_ref, sum_ref = refs[-2:]
    slots = weights_ref.shape[1]
    rows, _ = piece_refs[0].shape[1:]
    for step, piece_ref in zip(order, piece_refs):
        owner = jnp.bitwise_xor(me_ref[0], step)
        hold_ref[owner] = piece_ref[...].astype(F32)
    tile = min(rows, 8)
    for step, out_ref in zip(targets, out_refs):
        mom = jnp.bitwise_xor(me_ref[0], step)
        live = jnp.minimum(counts_ref[mom], slots)
        sum_ref[...] = jnp.zeros_like(sum_ref)

        def pair_step(pair, carry):
            entries = []
            for side in range(2):
                slot = jnp.minimum(2 * pair + side, slots - 1)
                moms = [triples_ref[mom, 3 * slot + place] for place in range(3)]
                factor = vertex_ref[weights_ref[mom, slot]]
                entries.append((moms, jnp.where(2 * pair + side < live, factor, 0.0)))
            for at in range(0, rows, tile):
                here = pl.ds(at, tile)
                total_re = sum_ref[0, here, :]
                total_im = sum_ref[1, here, :]
                for (first, second, third), factor in entries:
                    first_re = hold_ref[first, 0, here, :]
                    first_im = hold_ref[first, 1, here, :]
                    second_re = hold_ref[second, 0, here, :]
                    second_im = hold_ref[second, 1, here, :]
                    third_re = hold_ref[third, 0, here, :]
                    third_im = hold_ref[third, 1, here, :]
                    prod_re = first_re * second_re - first_im * second_im
                    prod_im = first_re * second_im + first_im * second_re
                    term_re = prod_re * third_re + prod_im * third_im
                    term_im = prod_im * third_re - prod_re * third_im
                    total_re = total_re + factor * term_re
                    total_im = total_im + factor * term_im
                sum_ref[0, here, :] = total_re
                sum_ref[1, here, :] = total_im
            return carry

        lax.fori_loop(0, (live + 1) // 2, pair_step, 0)
        out_ref[...] = sum_ref[...].astype(BF16)


def gather_kernel(order, me_ref, *refs):
    piece_refs = refs[:-1]
    out_ref = refs[-1]
    rows = piece_refs[0].shape[1]
    for step, piece_ref in zip(order, piece_refs):
        owner = jnp.bitwise_xor(me_ref[0], step)
        start = pl.multiple_of(owner * rows, rows)
        for part in range(2):
            out_ref[part, 0, pl.ds(start, rows), :] = piece_ref[part].astype(F32)


def step_order(moms):
    return sorted(range(1, moms), key=lambda step: (-step.bit_length(), step))


def local(source, inverse_diag, coupling, pair_moms, pair_count, pair_weight, vertex):
    size = inverse_diag.shape[3]
    columns = source.shape[3]
    widths = [columns * share // sum(SHARES) for share in SHARES]
    chunks = len(widths)
    moms = lax.axis_size("mom")
    times = lax.axis_size("tm")
    rows = size // moms
    me = lax.axis_index("mom").astype(jnp.int32).reshape(1)
    order = step_order(moms)
    smem = pl.BlockSpec(memory_space=pltpu.SMEM)
    vmem = pl.BlockSpec(memory_space=pltpu.VMEM)
    hbm = pl.BlockSpec(memory_space=pltpu.HBM)

    square = jax.ShapeDtypeStruct((2, size, size), F32)
    slabs = [jax.ShapeDtypeStruct((2, size, width), F32) for width in widths]
    outs = pl.pallas_call(
        load_kernel,
        out_shape=[slabs[0], square, square, *slabs[1:]],
        in_specs=[hbm] * 3,
        out_specs=[vmem] * (2 + chunks),
        scratch_shapes=[
            pltpu.VMEM((2, size, widths[0]), F32),
            pltpu.SemaphoreType.DMA((2 + chunks,)),
        ],
        compiler_params=params(16),
        cost_estimate=cost(24 * size * size * widths[0], 16 * size * columns),
        name="load",
    )(*(pltpu.with_memory_space_constraint(value, pltpu.HBM) for value in (inverse_diag, coupling, source)))
    inverse, coupled = outs[1:3]
    matrix = pl.pallas_call(
        propagator_kernel,
        out_shape=jax.ShapeDtypeStruct((2, 2, size, size), BF16),
        in_specs=[vmem] * 2,
        out_specs=vmem,
        compiler_params=params(16),
        cost_estimate=cost(24 * size**3, 8 * 4 * size * size),
        name="propagator",
    )(inverse, coupled)
    drive = [outs[0]]
    for chunk in range(1, chunks):
        drive.append(
            pl.pallas_call(
                drive_kernel,
                out_shape=slabs[chunk],
                in_specs=[vmem] * 2,
                out_specs=vmem,
                compiler_params=params(16),
                cost_estimate=cost(24 * size * size * widths[chunk], 16 * size * columns),
                name="drive",
            )(inverse, outs[2 + chunk])
        )

    def hop(state, incoming, dtypes):
        width = state.shape[-1]
        return pl.pallas_call(
            hop_kernel,
            out_shape=[jax.ShapeDtypeStruct((2, size, width), dtype) for dtype in dtypes],
            in_specs=[vmem] * 3,
            out_specs=[vmem] * len(dtypes),
            compiler_params=params(16),
            cost_estimate=cost(24 * size * size * width, 8 * 4 * size * width),
            name="hop",
        )(matrix, state, incoming)

    state = list(drive)
    sent = list(drive)
    arrived = [None] * chunks
    for turn in range(times - 1):
        for chunk in range(chunks):
            if turn:
                kinds = [F32] if turn % 2 == 0 else [F32, BF16]
                outs = hop(state[chunk], arrived[chunk], kinds)
                state[chunk], sent[chunk] = outs[0], outs[-1]
            arrived[chunk] = lax.ppermute(sent[chunk], "tm", [(turn, turn + 1)])

    ready = []
    for chunk in range(chunks - 1):
        ready.append(hop(state[chunk], arrived[chunk], [F32])[0])
    everyone = [*order, 0]
    piece = jax.ShapeDtypeStruct((2, rows, columns), BF16)
    *pieces, final = pl.pallas_call(
        functools.partial(last_kernel, everyone),
        out_shape=[piece] * moms + [slabs[-1]],
        in_specs=[smem] + [vmem] * (2 + chunks),
        out_specs=[vmem] * (1 + moms),
        compiler_params=params(16),
        cost_estimate=cost(24 * size * size * widths[-1], 8 * 4 * size * columns),
        name="last",
    )(me, matrix, state[-1], arrived[-1], *ready)
    solved = pl.pallas_call(
        emit_kernel,
        out_shape=jax.ShapeDtypeStruct((2, 1, size, columns), BF16),
        in_specs=[vmem] * chunks,
        out_specs=vmem,
        compiler_params=params(16),
        cost_estimate=cost(size * columns, 12 * size * columns),
        name="emit",
    )(*ready, final)

    def swap(value, step):
        return lax.ppermute(value, "mom", [(at, at ^ step) for at in range(moms)])

    arrived = [swap(value, step) for value, step in zip(pieces, order)] + [pieces[-1]]
    triples = pair_moms.reshape(pair_moms.shape[0], -1)

    def energy(targets):
        return pl.pallas_call(
            functools.partial(energy_kernel, everyone, targets),
            out_shape=[piece] * len(targets),
            in_specs=[smem] * 5 + [vmem] * moms,
            out_specs=[vmem] * len(targets),
            scratch_shapes=[
                pltpu.VMEM((moms, 2, rows, columns), F32),
                pltpu.VMEM((2, rows, columns), F32),
            ],
            compiler_params=params(16),
            cost_estimate=cost(100 * rows * columns * 8 * len(targets), 4 * size * columns),
            name="energy",
        )(me, triples, pair_count, pair_weight, vertex, *arrived)

    cut = moms // 4
    groups = [order[:cut], order[cut : 2 * cut], order[2 * cut :], [0]]
    home = []
    for targets in groups:
        values = energy(targets)
        for step, value in zip(targets, values):
            home.append(swap(value, step) if step else value)
    sigma = pl.pallas_call(
        functools.partial(gather_kernel, everyone),
        out_shape=jax.ShapeDtypeStruct((2, 1, size, columns), F32),
        in_specs=[smem] + [vmem] * moms,
        out_specs=vmem,
        compiler_params=params(16),
        cost_estimate=cost(size * columns, 12 * size * columns),
        name="gather",
    )(me, *home)
    return solved, sigma


def solution(mesh):
    return jax.shard_map(
        local,
        mesh=mesh,
        in_specs=(
            P(None, "mom", "tm", None),
            P(None, "mom", "tm", None, None),
            P(None, "mom", "tm", None, None),
            P(),
            P(),
            P(),
            P(),
        ),
        out_specs=(P(None, "mom", "tm", None), P(None, "mom", "tm", None)),
        check_vma=False,
    )
```

time: 63.9 us -> 61 us (0.955)
  waiting for transfers between devices: 19 us -> 17.4 us
  Pallas kernels: 14.5 us -> 13.3 us
    ppermute x14, waiting for transfers between devices: 12.6 us -> 10.9 us  [swap(): return lax.ppermute(value, 'mom', [(at, at ^ step) for at in range(moms)])]
    pallas_call x2 -> x4, Pallas kernels: 4.67 us -> 3.86 us  [the longest x1 1.82 us: local(): pl.pallas_call(load_kernel, out_shape=[slabs[0], square, square, *slabs[1...]
  transfers between devices with their start and end apart: 20 -> 20, of which waited for: 8 -> 7; matrix products, arithmetic and copies ran while one was open for 0% -> 0% of each run, Pallas kernels for 12% -> 14%
where the time goes in v1:
time: 61 us; the launch traced here: 60.8 us
  starting transfers between devices  29.2 us (48%)
  waiting for transfers between devices  17.4 us (29%)
  Pallas kernels  13.3 us (22%)
  between operations  0.88 us (1%)
    ppermute x14, starting transfers between devices, swap(): return lax.ppermute(value, 'mom', [(at, at ^ step) for at in range(moms)])  22.5 us
    ppermute x14, waiting for transfers between devices, swap(): return lax.ppermute(value, 'mom', [(at, at ^ step) for at in range(moms)])  10.9 us
    ppermute x6, starting transfers between devices, local(): arrived[chunk] = lax.ppermute(sent[chunk], 'tm', [(turn, turn + 1)])  6.62 us
    ppermute x6, waiting for transfers between devices, local(): arrived[chunk] = lax.ppermute(sent[chunk], 'tm', [(turn, turn + 1)])  6.41 us
    pallas_call x4, Pallas kernels, energy(): pl.pallas_call(functools.partial(energy_kernel, everyone, targets), out_s...  5.16 us
    pallas_call x5, Pallas kernels, hop(): pl.pallas_call(hop_kernel, out_shape=[jax.ShapeDtypeStruct((2, size, widt...  2.63 us
    pallas_call x1, Pallas kernels, local(): pl.pallas_call(load_kernel, out_shape=[slabs[0], square, square, *slabs[1...  1.82 us
  transfers between devices with their start and end apart: 20, of which 7 were waited for; matrix products, arithmetic and copies ran while one was open for 0% of the time, Pallas kernels for 14%

profile of v1, /device:TPU:4, one launch (start us, length us, event | category | flops | bytes accessed | tf_op | source)
XLA Modules:
  0.0 60.8 jit_solution(3506115606622257328)
XLA Ops:
  0.6 1.8 %load.1 = (f32[2,256,256]{2,1,0:T(8,128)S(1)}, f32[2,256,256]{2,1,0:T(8,128)S(1)}, f32[2,256,256]{2,1,0:T(8,128)S(1)}, f32[2,256,256]{2,1,0:T(8,128)S(1)}) custom-call(f32[2,1,1,256,256]{4,3,2,1,0:T(8,128)} %inverse_ref.1, f32[2,1,1,256,256]{4,3,2,1,0:T(8,128)} %coupling_ref.1, f32[2,1,256,512]{3,2,1,0:T(8,128)} %source_ref.1), custom_call_target="tpu_custom_call" | custom-call | flops 402653184 | bytes 2097152 | tf_op jit(solution)/shard_map/load/pallas_call | solution.py:219
  2.5 0.7 %collective-permute-start = (f32[2,256,256]{2,1,0:T(8,128)S(1)}, f32[2,256,256]{2,1,0:T(8,128)S(1)}, u32[]{:S(2)}, u32[]{:S(2)}) collective-permute-start(f32[2,256,256]{2,1,0:T(8,128)S(1)} %get-tuple-element.28.state_ref), channel_id=1, source_target_pairs={{0,1},{4,5},{8,9},{12,13},{16,17},{20,21},{24,25},{28,29}} | collective-permute-start | bytes 1572872 | tf_op jit(solution)/shard_map/ppermute | solution.py:277
  3.2 0.6 drive.1.state_ref
  3.8 0.7 %collective-permute-start.3 = (f32[2,256,256]{2,1,0:T(8,128)S(1)}, f32[2,256,256]{2,1,0:T(8,128)S(1)}, u32[]{:S(2)}, u32[]{:S(2)}) collective-permute-start(f32[2,256,256]{2,1,0:T(8,128)S(1)} %drive.1.state_ref), channel_id=1, source_target_pairs={{0,1},{4,5},{8,9},{12,13},{16,17},{20,21},{24,25},{28,29}} | collective-permute-start | bytes 1572872 | tf_op jit(solution)/shard_map/ppermute | solution.py:277
  4.5 0.6 propagator.1.matrix_ref
  5.1 0.6 hop.5
  5.7 1.3 %collective-permute-start.1 = (bf16[2,256,256]{2,1,0:T(8,128)(2,1)S(1)}, bf16[2,256,256]{2,1,0:T(8,128)(2,1)S(1)}, u32[]{:S(2)}, u32[]{:S(2)}) collective-permute-start(bf16[2,256,256]{2,1,0:T(8,128)(2,1)S(1)} %get-tuple-element.30), channel_id=1, source_target_pairs={{1,2},{5,6},{9,10},{13,14},{17,18},{21,22},{25,26},{29,30}} | collective-permute-start | bytes 786440 | tf_op jit(solution)/shard_map/ppermute | solution.py:277
  7.0 0.0 collective-permute-done.3.incoming_ref
  7.0 0.6 hop.8
  7.6 1.3 %collective-permute-start.4 = (bf16[2,256,256]{2,1,0:T(8,128)(2,1)S(1)}, bf16[2,256,256]{2,1,0:T(8,128)(2,1)S(1)}, u32[]{:S(2)}, u32[]{:S(2)}) collective-permute-start(bf16[2,256,256]{2,1,0:T(8,128)(2,1)S(1)} %get-tuple-element.33), channel_id=1, source_target_pairs={{1,2},{5,6},{9,10},{13,14},{17,18},{21,22},{25,26},{29,30}} | collective-permute-start | bytes 786440 | tf_op jit(solution)/shard_map/ppermute | solution.py:277
  8.9 4.5 %collective-permute-done.1.incoming_ref = bf16[2,256,256]{2,1,0:T(8,128)(2,1)S(1)} collective-permute-done((bf16[2,256,256]{2,1,0:T(8,128)(2,1)S(1)}, bf16[2,256,256]{2,1,0:T(8,128)(2,1)S(1)}, u32[]{:S(2)}, u32[]{:S(2)}) %collective-permute-start.1) | collective-permute-done | bytes 262176 | tf_op jit(solution)/shard_map/ppermute | solution.py:277
  13.3 0.4 hop.6.state_ref
  13.8 1.3 %collective-permute-start.2 = (f32[2,256,256]{2,1,0:T(8,128)S(1)}, f32[2,256,256]{2,1,0:T(8,128)S(1)}, u32[]{:S(2)}, u32[]{:S(2)}) collective-permute-start(f32[2,256,256]{2,1,0:T(8,128)S(1)} %hop.6.state_ref), channel_id=1, source_target_pairs={{2,3},{6,7},{10,11},{14,15},{18,19},{22,23},{26,27},{30,31}} | collective-permute-start | bytes 1572872 | tf_op jit(solution)/shard_map/ppermute | solution.py:277
  15.1 1.0 %collective-permute-done.4.incoming_ref = bf16[2,256,256]{2,1,0:T(8,128)(2,1)S(1)} collective-permute-done((bf16[2,256,256]{2,1,0:T(8,128)(2,1)S(1)}, bf16[2,256,256]{2,1,0:T(8,128)(2,1)S(1)}, u32[]{:S(2)}, u32[]{:S(2)}) %collective-permute-start.4) | collective-permute-done | bytes 262176 | tf_op jit(solution)/shard_map/ppermute | solution.py:277
  16.2 0.4 hop.9.state_ref
  16.6 1.3 %collective-permute-start.5 = (f32[2,256,256]{2,1,0:T(8,128)S(1)}, f32[2,256,256]{2,1,0:T(8,128)S(1)}, u32[]{:S(2)}, u32[]{:S(2)}) collective-permute-start(f32[2,256,256]{2,1,0:T(8,128)S(1)} %hop.9.state_ref), channel_id=1, source_target_pairs={{2,3},{6,7},{10,11},{14,15},{18,19},{22,23},{26,27},{30,31}} | collective-permute-start | bytes 1572872 | tf_op jit(solution)/shard_map/ppermute | solution.py:277
  17.9 0.0 collective-permute-done.2.incoming_ref
  17.9 0.6 hop.7.refs_0_
  18.5 0.9 %collective-permute-done.5.incoming_ref = f32[2,256,256]{2,1,0:T(8,128)S(1)} collective-permute-done((f32[2,256,256]{2,1,0:T(8,128)S(1)}, f32[2,256,256]{2,1,0:T(8,128)S(1)}, u32[]{:S(2)}, u32[]{:S(2)}) %collective-permute-start.5) | collective-permute-done | bytes 524320 | tf_op jit(solution)/shard_map/ppermute | solution.py:277
  19.4 0.6 last.1
  20.0 0.0 copy-start.3
  20.0 1.6 %collective-permute-start.10 = (bf16[2,32,512]{2,1,0:T(8,128)(2,1)S(1)}, bf16[2,32,512]{2,1,0:T(8,128)(2,1)S(1)}, u32[]{:S(2)}, u32[]{:S(2)}) collective-permute-start(bf16[2,32,512]{2,1,0:T(8,128)(2,1)S(1)} %get-tuple-element.39), channel_id=1, source_target_pairs={{0,8},{4,12},{8,0},{12,4},{16,24},{20,28},{24,16},{28,20},{1,9},{5... | collective-permute-start | bytes 196616 | tf_op jit(solution)/shard_map/ppermute | solution.py:304
  21.7 1.4 %collective-permute-start.11 = (bf16[2,32,512]{2,1,0:T(8,128)(2,1)S(1)}, bf16[2,32,512]{2,1,0:T(8,128)(2,1)S(1)}, u32[]{:S(2)}, u32[]{:S(2)}) collective-permute-start(bf16[2,32,512]{2,1,0:T(8,128)(2,1)S(1)} %get-tuple-element.40), channel_id=1, source_target_pairs={{0,12},{4,8},{8,4},{12,0},{16,28},{20,24},{24,20},{28,16},{1,13},{... | collective-permute-start | bytes 196616 | tf_op jit(solution)/shard_map/ppermute | solution.py:304
  23.1 0.5 collective-permute-start.12
  23.6 2.6 %collective-permute-start.6 = (bf16[2,32,512]{2,1,0:T(8,128)(2,1)S(1)}, bf16[2,32,512]{2,1,0:T(8,128)(2,1)S(1)}, u32[]{:S(2)}, u32[]{:S(2)}) collective-permute-start(bf16[2,32,512]{2,1,0:T(8,128)(2,1)S(1)} %get-tuple-element.35), channel_id=1, source_target_pairs={{0,16},{4,20},{8,24},{12,28},{16,0},{20,4},{24,8},{28,12},{1,17},{... | collective-permute-start | bytes 196616 | tf_op jit(solution)/shard_map/ppermute | solution.py:304
  26.2 1.3 %collective-permute-start.7 = (bf16[2,32,512]{2,1,0:T(8,128)(2,1)S(1)}, bf16[2,32,512]{2,1,0:T(8,128)(2,1)S(1)}, u32[]{:S(2)}, u32[]{:S(2)}) collective-permute-start(bf16[2,32,512]{2,1,0:T(8,128)(2,1)S(1)} %get-tuple-element.36), channel_id=1, source_target_pairs={{0,20},{4,16},{8,28},{12,24},{16,4},{20,0},{24,12},{28,8},{1,21},{... | collective-permute-start | bytes 196616 | tf_op jit(solution)/shard_map/ppermute | solution.py:304
  27.4 3.6 %collective-permute-start.8 = (bf16[2,32,512]{2,1,0:T(8,128)(2,1)S(1)}, bf16[2,32,512]{2,1,0:T(8,128)(2,1)S(1)}, u32[]{:S(2)}, u32[]{:S(2)}) collective-permute-start(bf16[2,32,512]{2,1,0:T(8,128)(2,1)S(1)} %get-tuple-element.37), channel_id=1, source_target_pairs={{0,24},{4,28},{8,16},{12,20},{16,8},{20,12},{24,0},{28,4},{1,25},{... | collective-permute-start | bytes 196616 | tf_op jit(solution)/shard_map/ppermute | solution.py:304
  31.1 0.2 collective-permute-start.9
  31.3 0.1 copy.10
  31.3 0.0 copy-start
  31.4 0.1 copy.11.triples_ref
  31.4 4.7 %collective-permute-done.7.refs_1_ = bf16[2,32,512]{2,1,0:T(8,128)(2,1)S(1)} collective-permute-done((bf16[2,32,512]{2,1,0:T(8,128)(2,1)S(1)}, bf16[2,32,512]{2,1,0:T(8,128)(2,1)S(1)}, u32[]{:S(2)}, u32[]{:S(2)}) %collective-permute-start.7) | collective-permute-done | bytes 65568 | tf_op jit(solution)/shard_map/ppermute | solution.py:304
  36.1 2.0 %collective-permute-done.9.refs_3_ = bf16[2,32,512]{2,1,0:T(8,128)(2,1)S(1)} collective-permute-done((bf16[2,32,512]{2,1,0:T(8,128)(2,1)S(1)}, bf16[2,32,512]{2,1,0:T(8,128)(2,1)S(1)}, u32[]{:S(2)}, u32[]{:S(2)}) %collective-permute-start.9) | collective-permute-done | bytes 65568 | tf_op jit(solution)/shard_map/ppermute | solution.py:304
  38.1 1.4 %energy.6 = (bf16[2,32,512]{2,1,0:T(8,128)(2,1)S(1)}, bf16[2,32,512]{2,1,0:T(8,128)(2,1)S(1)}, bf16[2,32,512]{2,1,0:T(8,128)(2,1)S(1)}) custom-call(s32[1]{0:T(128)} %bitcast.me_ref, s32[8,24]{1,0:T(8,128)S(1)} %copy.11.triples_ref, s32[8]{0:T(128)S(1)} %copy-done.1, s32[8,8]{1,0:T(8,128)S(1)} %copy-done, f32[16]{0:T(128)S(1)} %copy-done.2, ...), custom_call_target="tpu_custom_call" | custom-call | flops 39321600 | bytes 524288 | tf_op jit(solution)/shard_map/energy/pallas_call | solution.py:310
  39.5 1.9 %collective-permute-start.17 = (bf16[2,32,512]{2,1,0:T(8,128)(2,1)S(1)}, bf16[2,32,512]{2,1,0:T(8,128)(2,1)S(1)}, u32[]{:S(2)}, u32[]{:S(2)}) collective-permute-start(bf16[2,32,512]{2,1,0:T(8,128)(2,1)S(1)} %get-tuple-element.47), channel_id=1, source_target_pairs={{0,8},{4,12},{8,0},{12,4},{16,24},{20,28},{24,16},{28,20},{1,9},{5... | collective-permute-start | bytes 196616 | tf_op jit(solution)/shard_map/ppermute | solution.py:304
  41.4 0.4 collective-permute-start.18
  41.8 1.2 %collective-permute-start.19 = (bf16[2,32,512]{2,1,0:T(8,128)(2,1)S(1)}, bf16[2,32,512]{2,1,0:T(8,128)(2,1)S(1)}, u32[]{:S(2)}, u32[]{:S(2)}) collective-permute-start(bf16[2,32,512]{2,1,0:T(8,128)(2,1)S(1)} %get-tuple-element.49), channel_id=1, source_target_pairs={{0,4},{4,0},{8,12},{12,8},{16,20},{20,16},{24,28},{28,24},{1,5},{5... | collective-permute-start | bytes 196616 | tf_op jit(solution)/shard_map/ppermute | solution.py:304
  43.1 1.4 %energy.5 = (bf16[2,32,512]{2,1,0:T(8,128)(2,1)S(1)}, bf16[2,32,512]{2,1,0:T(8,128)(2,1)S(1)}) custom-call(s32[1]{0:T(128)} %bitcast.me_ref, s32[8,24]{1,0:T(8,128)S(1)} %copy.11.triples_ref, s32[8]{0:T(128)S(1)} %copy-done.1, s32[8,8]{1,0:T(8,128)S(1)} %copy-done, f32[16]{0:T(128)S(1)} %copy-done.2, bf16[2,32,512]{2,1,0:T(8,128)(2,1)S(1)} %collective-permute-done.6.refs_0_, ...), custom_call_target="tpu_custom_call" | custom-call | flops 26214400 | bytes 524288 | tf_op jit(solution)/shard_map/energy/pallas_call | solution.py:310
  44.5 3.1 %collective-permute-start.15 = (bf16[2,32,512]{2,1,0:T(8,128)(2,1)S(1)}, bf16[2,32,512]{2,1,0:T(8,128)(2,1)S(1)}, u32[]{:S(2)}, u32[]{:S(2)}) collective-permute-start(bf16[2,32,512]{2,1,0:T(8,128)(2,1)S(1)} %get-tuple-element.45), channel_id=1, source_target_pairs={{0,24},{4,28},{8,16},{12,20},{16,8},{20,12},{24,0},{28,4},{1,25},{... | collective-permute-start | bytes 196616 | tf_op jit(solution)/shard_map/ppermute | solution.py:304
  47.6 1.0 %collective-permute-start.16 = (bf16[2,32,512]{2,1,0:T(8,128)(2,1)S(1)}, bf16[2,32,512]{2,1,0:T(8,128)(2,1)S(1)}, u32[]{:S(2)}, u32[]{:S(2)}) collective-permute-start(bf16[2,32,512]{2,1,0:T(8,128)(2,1)S(1)} %get-tuple-element.46), channel_id=1, source_target_pairs={{0,28},{4,24},{8,20},{12,16},{16,12},{20,8},{24,4},{28,0},{1,29},{... | collective-permute-start | bytes 196616 | tf_op jit(solution)/shard_map/ppermute | solution.py:304
  48.6 1.2 %energy.4 = (bf16[2,32,512]{2,1,0:T(8,128)(2,1)S(1)}, bf16[2,32,512]{2,1,0:T(8,128)(2,1)S(1)}) custom-call(s32[1]{0:T(128)} %bitcast.me_ref, s32[8,24]{1,0:T(8,128)S(1)} %copy.11.triples_ref, s32[8]{0:T(128)S(1)} %copy-done.1, s32[8,8]{1,0:T(8,128)S(1)} %copy-done, f32[16]{0:T(128)S(1)} %copy-done.2, bf16[2,32,512]{2,1,0:T(8,128)(2,1)S(1)} %collective-permute-done.6.refs_0_, ...), custom_call_target="tpu_custom_call" | custom-call | flops 26214400 | bytes 524288 | tf_op jit(solution)/shard_map/energy/pallas_call | solution.py:310
  49.9 1.2 %collective-permute-start.13 = (bf16[2,32,512]{2,1,0:T(8,128)(2,1)S(1)}, bf16[2,32,512]{2,1,0:T(8,128)(2,1)S(1)}, u32[]{:S(2)}, u32[]{:S(2)}) collective-permute-start(bf16[2,32,512]{2,1,0:T(8,128)(2,1)S(1)} %get-tuple-element.43), channel_id=1, source_target_pairs={{0,16},{4,20},{8,24},{12,28},{16,0},{20,4},{24,8},{28,12},{1,17},{... | collective-permute-start | bytes 196616 | tf_op jit(solution)/shard_map/ppermute | solution.py:304
  51.1 2.4 %collective-permute-start.14 = (bf16[2,32,512]{2,1,0:T(8,128)(2,1)S(1)}, bf16[2,32,512]{2,1,0:T(8,128)(2,1)S(1)}, u32[]{:S(2)}, u32[]{:S(2)}) collective-permute-start(bf16[2,32,512]{2,1,0:T(8,128)(2,1)S(1)} %get-tuple-element.44), channel_id=1, source_target_pairs={{0,20},{4,16},{8,28},{12,24},{16,4},{20,0},{24,12},{28,8},{1,21},{... | collective-permute-start | bytes 196616 | tf_op jit(solution)/shard_map/ppermute | solution.py:304
  53.5 0.8 %emit.1 = bf16[2,1,256,512]{3,2,1,0:T(8,128)(2,1)} custom-call(f32[2,256,256]{2,1,0:T(8,128)S(1)} %hop.7.refs_0_, f32[2,256,256]{2,1,0:T(8,128)S(1)} %get-tuple-element.34.refs_1_), custom_call_target="tpu_custom_call" | custom-call | flops 131072 | bytes 1572864 | tf_op jit(solution)/shard_map/emit/pallas_call | solution.py:293
  54.4 1.1 %energy.7.refs_7_ = bf16[2,32,512]{2,1,0:T(8,128)(2,1)S(1)} custom-call(s32[1]{0:T(128)} %bitcast.me_ref, s32[8,24]{1,0:T(8,128)S(1)} %copy.11.triples_ref, s32[8]{0:T(128)S(1)} %copy-done.1, s32[8,8]{1,0:T(8,128)S(1)} %copy-done, f32[16]{0:T(128)S(1)} %copy-done.2, bf16[2,32,512]{2,1,0:T(8,128)(2,1)S(1)} %collective-permute-done.6.refs_0_, ...), custom_call_target="tpu_custom_call" | custom-call | flops 13107200 | bytes 524288 | tf_op jit(solution)/shard_map/energy/pallas_call | solution.py:310
  55.5 2.4 %collective-permute-done.13.refs_0_ = bf16[2,32,512]{2,1,0:T(8,128)(2,1)S(1)} collective-permute-done((bf16[2,32,512]{2,1,0:T(8,128)(2,1)S(1)}, bf16[2,32,512]{2,1,0:T(8,128)(2,1)S(1)}, u32[]{:S(2)}, u32[]{:S(2)}) %collective-permute-start.13) | collective-permute-done | bytes 65568 | tf_op jit(solution)/shard_map/ppermute | solution.py:304
  57.9 1.9 %collective-permute-done.14.refs_1_ = bf16[2,32,512]{2,1,0:T(8,128)(2,1)S(1)} collective-permute-done((bf16[2,32,512]{2,1,0:T(8,128)(2,1)S(1)}, bf16[2,32,512]{2,1,0:T(8,128)(2,1)S(1)}, u32[]{:S(2)}, u32[]{:S(2)}) %collective-permute-start.14) | collective-permute-done | bytes 65568 | tf_op jit(solution)/shard_map/ppermute | solution.py:304
  59.8 1.0 %gather.1 = f32[2,1,256,512]{3,2,1,0:T(8,128)} custom-call(s32[1]{0:T(128)} %bitcast.me_ref, bf16[2,32,512]{2,1,0:T(8,128)(2,1)S(1)} %collective-permute-done.13.refs_0_, bf16[2,32,512]{2,1,0:T(8,128)(2,1)S(1)} %collective-permute-done.14.refs_1_, bf16[2,32,512]{2,1,0:T(8,128)(2,1)S(1)} %collective-permute-done.15.refs_2_, ...), custom_call_target="tpu_custom_call" | custom-call | flops 131072 | bytes 1572864 | tf_op jit(solution)/shard_map/gather/pallas_call | solution.py:331
  (18 shorter events, 0.1 us)
Async XLA Ops:
  2.5 2.6 %collective-permute-start = (f32[2,256,256]{2,1,0:T(8,128)S(1)}, f32[2,256,256]{2,1,0:T(8,128)S(1)}, u32[]{:S(2)}, u32[]{:S(2)}) collective-permute-start(f32[2,256,256]{2,1,0:T(8,128)S(1)} %get-tuple-element.28.state_ref), channel_id=1, source_target_pairs={{0,1},{4,5},{8,9},{12,13},{16,17},{20,21},{24,25},{28,29}} | collective-permute-start | bytes 1572872 | tf_op jit(solution)/shard_map/ppermute | solution.py:277
  3.8 3.2 %collective-permute-start.3 = (f32[2,256,256]{2,1,0:T(8,128)S(1)}, f32[2,256,256]{2,1,0:T(8,128)S(1)}, u32[]{:S(2)}, u32[]{:S(2)}) collective-permute-start(f32[2,256,256]{2,1,0:T(8,128)S(1)} %drive.1.state_ref), channel_id=1, source_target_pairs={{0,1},{4,5},{8,9},{12,13},{16,17},{20,21},{24,25},{28,29}} | collective-permute-start | bytes 1572872 | tf_op jit(solution)/shard_map/ppermute | solution.py:277
  5.7 7.7 %collective-permute-start.1 = (bf16[2,256,256]{2,1,0:T(8,128)(2,1)S(1)}, bf16[2,256,256]{2,1,0:T(8,128)(2,1)S(1)}, u32[]{:S(2)}, u32[]{:S(2)}) collective-permute-start(bf16[2,256,256]{2,1,0:T(8,128)(2,1)S(1)} %get-tuple-element.30), channel_id=1, source_target_pairs={{1,2},{5,6},{9,10},{13,14},{17,18},{21,22},{25,26},{29,30}} | collective-permute-start | bytes 786440 | tf_op jit(solution)/shard_map/ppermute | solution.py:277
  7.6 8.6 %collective-permute-start.4 = (bf16[2,256,256]{2,1,0:T(8,128)(2,1)S(1)}, bf16[2,256,256]{2,1,0:T(8,128)(2,1)S(1)}, u32[]{:S(2)}, u32[]{:S(2)}) collective-permute-start(bf16[2,256,256]{2,1,0:T(8,128)(2,1)S(1)} %get-tuple-element.33), channel_id=1, source_target_pairs={{1,2},{5,6},{9,10},{13,14},{17,18},{21,22},{25,26},{29,30}} | collective-permute-start | bytes 786440 | tf_op jit(solution)/shard_map/ppermute | solution.py:277
  13.8 4.1 %collective-permute-start.2 = (f32[2,256,256]{2,1,0:T(8,128)S(1)}, f32[2,256,256]{2,1,0:T(8,128)S(1)}, u32[]{:S(2)}, u32[]{:S(2)}) collective-permute-start(f32[2,256,256]{2,1,0:T(8,128)S(1)} %hop.6.state_ref), channel_id=1, source_target_pairs={{2,3},{6,7},{10,11},{14,15},{18,19},{22,23},{26,27},{30,31}} | collective-permute-start | bytes 1572872 | tf_op jit(solution)/shard_map/ppermute | solution.py:277
  16.6 2.8 %collective-permute-start.5 = (f32[2,256,256]{2,1,0:T(8,128)S(1)}, f32[2,256,256]{2,1,0:T(8,128)S(1)}, u32[]{:S(2)}, u32[]{:S(2)}) collective-permute-start(f32[2,256,256]{2,1,0:T(8,128)S(1)} %hop.9.state_ref), channel_id=1, source_target_pairs={{2,3},{6,7},{10,11},{14,15},{18,19},{22,23},{26,27},{30,31}} | collective-permute-start | bytes 1572872 | tf_op jit(solution)/shard_map/ppermute | solution.py:277
  20.0 11.2 %copy-start.3 = (s32[8,8,3]{1,0,2:T(8,128)S(1)}, s32[8,8,3]{1,0,2:T(8,128)}, u32[]{:S(2)}) copy-start(s32[8,8,3]{1,0,2:T(8,128)} %param.10) | copy-start | bytes 2308
  20.0 7.4 %collective-permute-start.10 = (bf16[2,32,512]{2,1,0:T(8,128)(2,1)S(1)}, bf16[2,32,512]{2,1,0:T(8,128)(2,1)S(1)}, u32[]{:S(2)}, u32[]{:S(2)}) collective-permute-start(bf16[2,32,512]{2,1,0:T(8,128)(2,1)S(1)} %get-tuple-element.39), channel_id=1, source_target_pairs={{0,8},{4,12},{8,0},{12,4},{16,24},{20,28},{24,16},{28,20},{1,9},{5... | collective-permute-start | bytes 196616 | tf_op jit(solution)/shard_map/ppermute | solution.py:304
  21.7 9.4 %collective-permute-start.11 = (bf16[2,32,512]{2,1,0:T(8,128)(2,1)S(1)}, bf16[2,32,512]{2,1,0:T(8,128)(2,1)S(1)}, u32[]{:S(2)}, u32[]{:S(2)}) collective-permute-start(bf16[2,32,512]{2,1,0:T(8,128)(2,1)S(1)} %get-tuple-element.40), channel_id=1, source_target_pairs={{0,12},{4,8},{8,4},{12,0},{16,28},{20,24},{24,20},{28,16},{1,13},{... | collective-permute-start | bytes 196616 | tf_op jit(solution)/shard_map/ppermute | solution.py:304
  23.1 8.4 %collective-permute-start.12 = (bf16[2,32,512]{2,1,0:T(8,128)(2,1)S(1)}, bf16[2,32,512]{2,1,0:T(8,128)(2,1)S(1)}, u32[]{:S(2)}, u32[]{:S(2)}) collective-permute-start(bf16[2,32,512]{2,1,0:T(8,128)(2,1)S(1)} %get-tuple-element.41), channel_id=1, source_target_pairs={{0,4},{4,0},{8,12},{12,8},{16,20},{20,16},{24,28},{28,24},{1,5},{5... | collective-permute-start | bytes 196616 | tf_op jit(solution)/shard_map/ppermute | solution.py:304
  23.6 7.8 %collective-permute-start.6 = (bf16[2,32,512]{2,1,0:T(8,128)(2,1)S(1)}, bf16[2,32,512]{2,1,0:T(8,128)(2,1)S(1)}, u32[]{:S(2)}, u32[]{:S(2)}) collective-permute-start(bf16[2,32,512]{2,1,0:T(8,128)(2,1)S(1)} %get-tuple-element.35), channel_id=1, source_target_pairs={{0,16},{4,20},{8,24},{12,28},{16,0},{20,4},{24,8},{28,12},{1,17},{... | collective-permute-start | bytes 196616 | tf_op jit(solution)/shard_map/ppermute | solution.py:304
  26.2 10.0 %collective-permute-start.7 = (bf16[2,32,512]{2,1,0:T(8,128)(2,1)S(1)}, bf16[2,32,512]{2,1,0:T(8,128)(2,1)S(1)}, u32[]{:S(2)}, u32[]{:S(2)}) collective-permute-start(bf16[2,32,512]{2,1,0:T(8,128)(2,1)S(1)} %get-tuple-element.36), channel_id=1, source_target_pairs={{0,20},{4,16},{8,28},{12,24},{16,4},{20,0},{24,12},{28,8},{1,21},{... | collective-permute-start | bytes 196616 | tf_op jit(solution)/shard_map/ppermute | solution.py:304
  27.4 8.7 %collective-permute-start.8 = (bf16[2,32,512]{2,1,0:T(8,128)(2,1)S(1)}, bf16[2,32,512]{2,1,0:T(8,128)(2,1)S(1)}, u32[]{:S(2)}, u32[]{:S(2)}) collective-permute-start(bf16[2,32,512]{2,1,0:T(8,128)(2,1)S(1)} %get-tuple-element.37), channel_id=1, source_target_pairs={{0,24},{4,28},{8,16},{12,20},{16,8},{20,12},{24,0},{28,4},{1,25},{... | collective-permute-start | bytes 196616 | tf_op jit(solution)/shard_map/ppermute | solution.py:304
  31.1 7.1 %collective-permute-start.9 = (bf16[2,32,512]{2,1,0:T(8,128)(2,1)S(1)}, bf16[2,32,512]{2,1,0:T(8,128)(2,1)S(1)}, u32[]{:S(2)}, u32[]{:S(2)}) collective-permute-start(bf16[2,32,512]{2,1,0:T(8,128)(2,1)S(1)} %get-tuple-element.38), channel_id=1, source_target_pairs={{0,28},{4,24},{8,20},{12,16},{16,12},{20,8},{24,4},{28,0},{1,29},{... | collective-permute-start | bytes 196616 | tf_op jit(solution)/shard_map/ppermute | solution.py:304
  31.3 6.8 %copy-start = (s32[8,8]{1,0:T(8,128)S(1)}, s32[8,8]{1,0:T(8,128)}, u32[]{:S(2)}) copy-start(s32[8,8]{1,0:T(8,128)} %weights_ref.7) | copy-start | bytes 772
  31.4 6.7 %copy-start.1 = (s32[8]{0:T(128)S(1)}, s32[8]{0:T(128)}, u32[]{:S(2)}) copy-start(s32[8]{0:T(128)} %counts_ref.7) | copy-start | bytes 100
  31.4 6.7 %copy-start.2 = (f32[16]{0:T(128)S(1)}, f32[16]{0:T(128)}, u32[]{:S(2)}) copy-start(f32[16]{0:T(128)} %vertex_ref.7) | copy-start | bytes 196
  39.5 10.4 %collective-permute-start.17 = (bf16[2,32,512]{2,1,0:T(8,128)(2,1)S(1)}, bf16[2,32,512]{2,1,0:T(8,128)(2,1)S(1)}, u32[]{:S(2)}, u32[]{:S(2)}) collective-permute-start(bf16[2,32,512]{2,1,0:T(8,128)(2,1)S(1)} %get-tuple-element.47), channel_id=1, source_target_pairs={{0,8},{4,12},{8,0},{12,4},{16,24},{20,28},{24,16},{28,20},{1,9},{5... | collective-permute-start | bytes 196616 | tf_op jit(solution)/shard_map/ppermute | solution.py:304
  41.4 9.7 %collective-permute-start.18 = (bf16[2,32,512]{2,1,0:T(8,128)(2,1)S(1)}, bf16[2,32,512]{2,1,0:T(8,128)(2,1)S(1)}, u32[]{:S(2)}, u32[]{:S(2)}) collective-permute-start(bf16[2,32,512]{2,1,0:T(8,128)(2,1)S(1)} %get-tuple-element.48), channel_id=1, source_target_pairs={{0,12},{4,8},{8,4},{12,0},{16,28},{20,24},{24,20},{28,16},{1,13},{... | collective-permute-start | bytes 196616 | tf_op jit(solution)/shard_map/ppermute | solution.py:304
  41.8 13.7 %collective-permute-start.19 = (bf16[2,32,512]{2,1,0:T(8,128)(2,1)S(1)}, bf16[2,32,512]{2,1,0:T(8,128)(2,1)S(1)}, u32[]{:S(2)}, u32[]{:S(2)}) collective-permute-start(bf16[2,32,512]{2,1,0:T(8,128)(2,1)S(1)} %get-tuple-element.49), channel_id=1, source_target_pairs={{0,4},{4,0},{8,12},{12,8},{16,20},{20,16},{24,28},{28,24},{1,5},{5... | collective-permute-start | bytes 196616 | tf_op jit(solution)/shard_map/ppermute | solution.py:304
  44.5 11.0 %collective-permute-start.15 = (bf16[2,32,512]{2,1,0:T(8,128)(2,1)S(1)}, bf16[2,32,512]{2,1,0:T(8,128)(2,1)S(1)}, u32[]{:S(2)}, u32[]{:S(2)}) collective-permute-start(bf16[2,32,512]{2,1,0:T(8,128)(2,1)S(1)} %get-tuple-element.45), channel_id=1, source_target_pairs={{0,24},{4,28},{8,16},{12,20},{16,8},{20,12},{24,0},{28,4},{1,25},{... | collective-permute-start | bytes 196616 | tf_op jit(solution)/shard_map/ppermute | solution.py:304
  47.6 7.9 %collective-permute-start.16 = (bf16[2,32,512]{2,1,0:T(8,128)(2,1)S(1)}, bf16[2,32,512]{2,1,0:T(8,128)(2,1)S(1)}, u32[]{:S(2)}, u32[]{:S(2)}) collective-permute-start(bf16[2,32,512]{2,1,0:T(8,128)(2,1)S(1)} %get-tuple-element.46), channel_id=1, source_target_pairs={{0,28},{4,24},{8,20},{12,16},{16,12},{20,8},{24,4},{28,0},{1,29},{... | collective-permute-start | bytes 196616 | tf_op jit(solution)/shard_map/ppermute | solution.py:304
  49.9 8.0 %collective-permute-start.13 = (bf16[2,32,512]{2,1,0:T(8,128)(2,1)S(1)}, bf16[2,32,512]{2,1,0:T(8,128)(2,1)S(1)}, u32[]{:S(2)}, u32[]{:S(2)}) collective-permute-start(bf16[2,32,512]{2,1,0:T(8,128)(2,1)S(1)} %get-tuple-element.43), channel_id=1, source_target_pairs={{0,16},{4,20},{8,24},{12,28},{16,0},{20,4},{24,8},{28,12},{1,17},{... | collective-permute-start | bytes 196616 | tf_op jit(solution)/shard_map/ppermute | solution.py:304
  51.1 8.7 %collective-permute-start.14 = (bf16[2,32,512]{2,1,0:T(8,128)(2,1)S(1)}, bf16[2,32,512]{2,1,0:T(8,128)(2,1)S(1)}, u32[]{:S(2)}, u32[]{:S(2)}) collective-permute-start(bf16[2,32,512]{2,1,0:T(8,128)(2,1)S(1)} %get-tuple-element.44), channel_id=1, source_target_pairs={{0,20},{4,16},{8,28},{12,24},{16,4},{20,0},{24,12},{28,8},{1,21},{... | collective-permute-start | bytes 196616 | tf_op jit(solution)/shard_map/ppermute | solution.py:304

commit v2 on v1

--- a/solution.py
+++ b/solution.py
@@ -97,24 +97,33 @@
     return dot_split(high, low, *split(stacked))
 
 
-def hop_kernel(matrix_ref, state_ref, incoming_ref, *out_refs):
+def hop_kernel(turn, at_ref, matrix_ref, state_ref, incoming_ref, *out_refs):
     size = state_ref.shape[1]
-    result = advance(matrix_ref, incoming_ref)
-    for part in range(2):
-        value = state_ref[part] + result[part * size : (part + 1) * size]
-        for out_ref in out_refs:
-            out_ref[part] = value.astype(out_ref.dtype)
-
-
-def last_kernel(order, me_ref, matrix_ref, state_ref, incoming_ref, *refs):
+
+    @pl.when(at_ref[0] == turn)
+    def receive():
+        result = advance(matrix_ref, incoming_ref)
+        for part in range(2):
+            value = state_ref[part] + result[part * size : (part + 1) * size]
+            for out_ref in out_refs:
+                out_ref[part] = value.astype(out_ref.dtype)
+
+    @pl.when(at_ref[0] != turn)
+    def keep():
+        out_refs[0][...] = state_ref[...]
+
+
+def table_kernel(*refs):
+    for at in range(len(refs) // 2):
+        refs[len(refs) // 2 + at][...] = refs[at][...]
+
+
+def last_kernel(order, turn, me_ref, at_ref, matrix_ref, state_ref, incoming_ref, *refs):
     chunks = len(refs) - len(order)
     ready_refs = refs[: chunks - 1]
     piece_refs = refs[chunks - 1 : -1]
     hold_ref = refs[-1]
-    size, _ = state_ref.shape[1:]
-    result = advance(matrix_ref, incoming_ref)
-    for part in range(2):
-        hold_ref[part] = state_ref[part] + result[part * size : (part + 1) * size]
+    hop_kernel(turn, at_ref, matrix_ref, state_ref, incoming_ref, hold_ref)
     rows = piece_refs[0].shape[1]
     first = 0
     for ref in [*ready_refs, hold_ref]:
@@ -137,20 +146,29 @@
             solved_ref[part, 0, :, columns] = ref[part].astype(BF16)
 
 
-def energy_kernel(order, targets, me_ref, triples_ref, counts_ref, weights_ref, vertex_ref, *refs):
+def energy_kernel(order, targets, me_ref, *refs):
     count = len(order)
-    piece_refs = refs[:count]
-    out_refs = refs[count:-2]
-    hold_ref, sum_ref = refs[-2:]
+    piece_refs = refs[4 : 4 + count]
+    out_refs = refs[4 + count : -7]
+    hold_ref, sum_ref, *tables, sems = refs[-7:]
+    copies = [
+        pltpu.make_async_copy(origin, target, sems.at[at])
+        for at, (origin, target) in enumerate(zip(refs[:4], tables))
+    ]
+    for copy in copies:
+        copy.start()
+    triples_ref, counts_ref, weights_ref, vertex_ref = tables
     slots = weights_ref.shape[1]
     rows, _ = piece_refs[0].shape[1:]
     for step, piece_ref in zip(order, piece_refs):
         owner = jnp.bitwise_xor(me_ref[0], step)
         hold_ref[owner] = piece_ref[...].astype(F32)
+    for copy in copies:
+        copy.wait()
     tile = min(rows, 8)
     for step, out_ref in zip(targets, out_refs):
         mom = jnp.bitwise_xor(me_ref[0], step)
-        live = jnp.minimum(counts_ref[mom], slots)
+        live = jnp.minimum(counts_ref[0, mom], slots)
         sum_ref[...] = jnp.zeros_like(sum_ref)
 
         def pair_step(pair, carry):
@@ -158,7 +176,7 @@
             for side in range(2):
                 slot = jnp.minimum(2 * pair + side, slots - 1)
                 moms = [triples_ref[mom, 3 * slot + place] for place in range(3)]
-                factor = vertex_ref[weights_ref[mom, slot]]
+                factor = vertex_ref[0, weights_ref[mom, slot]]
                 entries.append((moms, jnp.where(2 * pair + side < live, factor, 0.0)))
             for at in range(0, rows, tile):
                 here = pl.ds(at, tile)
@@ -253,17 +271,20 @@
             )(inverse, outs[2 + chunk])
         )
 
-    def hop(state, incoming, dtypes):
+    at = lax.axis_index("tm").astype(jnp.int32).reshape(1)
+
+    def hop(turn, state, incoming, dtypes):
         width = state.shape[-1]
         return pl.pallas_call(
-            hop_kernel,
+            functools.partial(hop_kernel, turn),
             out_shape=[jax.ShapeDtypeStruct((2, size, width), dtype) for dtype in dtypes],
-            in_specs=[vmem] * 3,
+            in_specs=[smem] + [vmem] * 3,
             out_specs=[vmem] * len(dtypes),
+            input_output_aliases={2: 0},
             compiler_params=params(16),
             cost_estimate=cost(24 * size * size * width, 8 * 4 * size * width),
             name="hop",
-        )(matrix, state, incoming)
+        )(at, matrix, state, incoming)
 
     state = list(drive)
     sent = list(drive)
@@ -272,24 +293,25 @@
         for chunk in range(chunks):
             if turn:
                 kinds = [F32] if turn % 2 == 0 else [F32, BF16]
-                outs = hop(state[chunk], arrived[chunk], kinds)
+                outs = hop(turn, state[chunk], arrived[chunk], kinds)
                 state[chunk], sent[chunk] = outs[0], outs[-1]
             arrived[chunk] = lax.ppermute(sent[chunk], "tm", [(turn, turn + 1)])
 
     ready = []
     for chunk in range(chunks - 1):
-        ready.append(hop(state[chunk], arrived[chunk], [F32])[0])
+        ready.append(hop(times - 1, state[chunk], arrived[chunk], [F32])[0])
     everyone = [*order, 0]
     piece = jax.ShapeDtypeStruct((2, rows, columns), BF16)
     *pieces, final = pl.pallas_call(
-        functools.partial(last_kernel, everyone),
+        functools.partial(last_kernel, everyone, times - 1),
         out_shape=[piece] * moms + [slabs[-1]],
-        in_specs=[smem] + [vmem] * (2 + chunks),
+        in_specs=[smem] * 2 + [vmem] * (2 + chunks),
         out_specs=[vmem] * (1 + moms),
+        input_output_aliases={3: moms},
         compiler_params=params(16),
         cost_estimate=cost(24 * size * size * widths[-1], 8 * 4 * size * columns),
         name="last",
-    )(me, matrix, state[-1], arrived[-1], *ready)
+    )(me, at, matrix, state[-1], arrived[-1], *ready)
     solved = pl.pallas_call(
         emit_kernel,
         out_shape=jax.ShapeDtypeStruct((2, 1, size, columns), BF16),
@@ -304,25 +326,41 @@
         return lax.ppermute(value, "mom", [(at, at ^ step) for at in range(moms)])
 
     arrived = [swap(value, step) for value, step in zip(pieces, order)] + [pieces[-1]]
-    triples = pair_moms.reshape(pair_moms.shape[0], -1)
+    tables = (
+        pair_moms.reshape(pair_moms.shape[0], -1),
+        pair_count.reshape(1, -1),
+        pair_weight,
+        vertex.reshape(1, -1),
+    )
+    tables = pl.pallas_call(
+        table_kernel,
+        out_shape=[jax.ShapeDtypeStruct(table.shape, table.dtype) for table in tables],
+        in_specs=[vmem] * len(tables),
+        out_specs=[vmem] * len(tables),
+        compiler_params=params(16),
+        name="tables",
+    )(*tables)
 
     def energy(targets):
         return pl.pallas_call(
             functools.partial(energy_kernel, everyone, targets),
             out_shape=[piece] * len(targets),
-            in_specs=[smem] * 5 + [vmem] * moms,
+            in_specs=[smem] + [vmem] * (4 + moms),
             out_specs=[vmem] * len(targets),
             scratch_shapes=[
                 pltpu.VMEM((moms, 2, rows, columns), F32),
                 pltpu.VMEM((2, rows, columns), F32),
+                *(pltpu.SMEM(table.shape, table.dtype) for table in tables),
+                pltpu.SemaphoreType.DMA((4,)),
             ],
             compiler_params=params(16),
             cost_estimate=cost(100 * rows * columns * 8 * len(targets), 4 * size * columns),
             name="energy",
-        )(me, triples, pair_count, pair_weight, vertex, *arrived)
+        )(me, *tables, *arrived)
 
     cut = moms // 4
-    groups = [order[:cut], order[cut : 2 * cut], order[2 * cut :], [0]]
+    lead = max(1, cut // 2)
+    groups = [order[:lead], order[lead : 2 * cut], order[2 * cut :], [0]]
     home = []
     for targets in groups:
         values = energy(targets)

time: 61 us -> 62.1 us (1.018)
  starting transfers between devices: 29.2 us -> 30.9 us
  Pallas kernels: 13.3 us -> 12.2 us
  local copies, waits for them, and re-layouts: 0.17 us -> 0.84 us
    ppermute x14, waiting for transfers between devices: 10.9 us -> 9.58 us  [swap(): return lax.ppermute(value, 'mom', [(at, at ^ step) for at in range(moms)])]
    ppermute x6, waiting for transfers between devices: 6.41 us -> 7.4 us  [local(): arrived[chunk] = lax.ppermute(sent[chunk], 'tm', [(turn, turn + 1)])]
    ppermute x14, starting transfers between devices: 22.5 us -> 23.5 us  [swap(): return lax.ppermute(value, 'mom', [(at, at ^ step) for at in range(moms)])]
    pallas_call x6 -> x7, Pallas kernels: 3.23 us -> 2.31 us  [the longest x5 2.19 us: hop(): pl.pallas_call(functools.partial(hop_kernel, turn), out_shape=[jax.ShapeD...]
    ppermute x6, starting transfers between devices: 6.62 us -> 7.42 us  [local(): arrived[chunk] = lax.ppermute(sent[chunk], 'tm', [(turn, turn + 1)])]
    unnamed x9, local copies, waits for them, and re-layouts: 0.09 us -> 0.76 us
  transfers between devices with their start and end apart: 20 -> 20, of which waited for: 7 -> 7; matrix products, arithmetic and copies ran while one was open for 0% -> 0% of each run, Pallas kernels for 14% -> 13%
where the time goes in v2:
time: 62.1 us; the launch traced here: 61.8 us
  starting transfers between devices  30.9 us (50%)
  waiting for transfers between devices  17 us (27%)
  Pallas kernels  12.2 us (20%)
  between operations  0.87 us (1%)
  local copies, waits for them, and re-layouts  0.84 us (1%)
    ppermute x14, starting transfers between devices, swap(): return lax.ppermute(value, 'mom', [(at, at ^ step) for at in range(moms)])  23.5 us
    ppermute x14, waiting for transfers between devices, swap(): return lax.ppermute(value, 'mom', [(at, at ^ step) for at in range(moms)])  9.58 us
    ppermute x6, starting transfers between devices, local(): arrived[chunk] = lax.ppermute(sent[chunk], 'tm', [(turn, turn + 1)])  7.42 us
    ppermute x6, waiting for transfers between devices, local(): arrived[chunk] = lax.ppermute(sent[chunk], 'tm', [(turn, turn + 1)])  7.4 us
    pallas_call x4, Pallas kernels, energy(): pl.pallas_call(functools.partial(energy_kernel, everyone, targets), out_s...  5.05 us
    pallas_call x5, Pallas kernels, hop(): pl.pallas_call(functools.partial(hop_kernel, turn), out_shape=[jax.ShapeD...  2.19 us
    pallas_call x1, Pallas kernels, local(): pl.pallas_call(load_kernel, out_shape=[slabs[0], square, square, *slabs[1...  1.82 us
  transfers between devices with their start and end apart: 20, of which 7 were waited for; matrix products, arithmetic and copies ran while one was open for 0% of the time, Pallas kernels for 13%

profile of v2, /device:TPU:4, one launch (start us, length us, event | category | flops | bytes accessed | tf_op | source)
XLA Modules:
  0.0 61.8 jit_solution(16970927890558548433)
XLA Ops:
  0.6 1.8 %load.1 = (f32[2,256,256]{2,1,0:T(8,128)S(1)}, f32[2,256,256]{2,1,0:T(8,128)S(1)}, f32[2,256,256]{2,1,0:T(8,128)S(1)}, f32[2,256,256]{2,1,0:T(8,128)S(1)}) custom-call(f32[2,1,1,256,256]{4,3,2,1,0:T(8,128)} %inverse_ref.1, f32[2,1,1,256,256]{4,3,2,1,0:T(8,128)} %coupling_ref.1, f32[2,1,256,512]{3,2,1,0:T(8,128)} %source_ref.1), custom_call_target="tpu_custom_call" | custom-call | flops 402653184 | bytes 2097152 | tf_op jit(solution)/shard_map/load/pallas_call | solution.py:237
  2.5 1.5 %collective-permute-start = (f32[2,256,256]{2,1,0:T(8,128)S(1)}, f32[2,256,256]{2,1,0:T(8,128)}, u32[]{:S(2)}, u32[]{:S(2)}) collective-permute-start(f32[2,256,256]{2,1,0:T(8,128)S(1)} %get-tuple-element.31.state_ref), channel_id=1, source_target_pairs={{0,1},{4,5},{8,9},{12,13},{16,17},{20,21},{24,25},{28,29}} | collective-permute-start | bytes 1572872 | tf_op jit(solution)/shard_map/ppermute | solution.py:298
  4.0 0.6 drive.1.state_ref
  4.5 0.7 %collective-permute-start.3 = (f32[2,256,256]{2,1,0:T(8,128)S(1)}, f32[2,256,256]{2,1,0:T(8,128)S(1)}, u32[]{:S(2)}, u32[]{:S(2)}) collective-permute-start(f32[2,256,256]{2,1,0:T(8,128)S(1)} %drive.1.state_ref), channel_id=1, source_target_pairs={{0,1},{4,5},{8,9},{12,13},{16,17},{20,21},{24,25},{28,29}} | collective-permute-start | bytes 1572872 | tf_op jit(solution)/shard_map/ppermute | solution.py:298
  5.2 0.6 propagator.1.matrix_ref
  5.9 1.1 %hop.5 = (f32[2,256,256]{2,1,0:T(8,128)S(1)}, bf16[2,256,256]{2,1,0:T(8,128)(2,1)S(1)}) custom-call(s32[1]{0:T(128)} %bitcast.at_ref, bf16[2,2,256,256]{3,2,1,0:T(8,128)(2,1)S(1)} %propagator.1.matrix_ref, f32[2,256,256]{2,1,0:T(8,128)S(1)} %get-tuple-element.31.state_ref, ...), custom_call_target="tpu_custom_call", output_to_operand_aliasing={{0}: (2, {})} | custom-call | flops 402653184 | bytes 2097152 | tf_op jit(solution)/shard_map/hop/pallas_call | solution.py:278
  7.0 1.3 %collective-permute-start.1 = (bf16[2,256,256]{2,1,0:T(8,128)(2,1)S(1)}, bf16[2,256,256]{2,1,0:T(8,128)(2,1)S(1)}, u32[]{:S(2)}, u32[]{:S(2)}) collective-permute-start(bf16[2,256,256]{2,1,0:T(8,128)(2,1)S(1)} %get-tuple-element.33), channel_id=1, source_target_pairs={{1,2},{5,6},{9,10},{13,14},{17,18},{21,22},{25,26},{29,30}} | collective-permute-start | bytes 786440 | tf_op jit(solution)/shard_map/ppermute | solution.py:298
  8.3 0.1 hop.8
  8.4 1.3 %collective-permute-start.4 = (bf16[2,256,256]{2,1,0:T(8,128)(2,1)S(1)}, bf16[2,256,256]{2,1,0:T(8,128)(2,1)S(1)}, u32[]{:S(2)}, u32[]{:S(2)}) collective-permute-start(bf16[2,256,256]{2,1,0:T(8,128)(2,1)S(1)} %get-tuple-element.36), channel_id=1, source_target_pairs={{1,2},{5,6},{9,10},{13,14},{17,18},{21,22},{25,26},{29,30}} | collective-permute-start | bytes 786440 | tf_op jit(solution)/shard_map/ppermute | solution.py:298
  9.7 5.0 %collective-permute-done.1.incoming_ref = bf16[2,256,256]{2,1,0:T(8,128)(2,1)S(1)} collective-permute-done((bf16[2,256,256]{2,1,0:T(8,128)(2,1)S(1)}, bf16[2,256,256]{2,1,0:T(8,128)(2,1)S(1)}, u32[]{:S(2)}, u32[]{:S(2)}) %collective-permute-start.1) | collective-permute-done | bytes 262176 | tf_op jit(solution)/shard_map/ppermute | solution.py:298
  14.7 0.5 hop.6.state_ref
  15.1 1.3 %collective-permute-start.2 = (f32[2,256,256]{2,1,0:T(8,128)S(1)}, f32[2,256,256]{2,1,0:T(8,128)S(1)}, u32[]{:S(2)}, u32[]{:S(2)}) collective-permute-start(f32[2,256,256]{2,1,0:T(8,128)S(1)} %hop.6.state_ref), channel_id=1, source_target_pairs={{2,3},{6,7},{10,11},{14,15},{18,19},{22,23},{26,27},{30,31}} | collective-permute-start | bytes 1572872 | tf_op jit(solution)/shard_map/ppermute | solution.py:298
  16.5 1.0 %collective-permute-done.4.incoming_ref = bf16[2,256,256]{2,1,0:T(8,128)(2,1)S(1)} collective-permute-done((bf16[2,256,256]{2,1,0:T(8,128)(2,1)S(1)}, bf16[2,256,256]{2,1,0:T(8,128)(2,1)S(1)}, u32[]{:S(2)}, u32[]{:S(2)}) %collective-permute-start.4) | collective-permute-done | bytes 262176 | tf_op jit(solution)/shard_map/ppermute | solution.py:298
  17.5 0.5 hop.9.state_ref
  17.9 1.3 %collective-permute-start.5 = (f32[2,256,256]{2,1,0:T(8,128)S(1)}, f32[2,256,256]{2,1,0:T(8,128)S(1)}, u32[]{:S(2)}, u32[]{:S(2)}) collective-permute-start(f32[2,256,256]{2,1,0:T(8,128)S(1)} %hop.9.state_ref), channel_id=1, source_target_pairs={{2,3},{6,7},{10,11},{14,15},{18,19},{22,23},{26,27},{30,31}} | collective-permute-start | bytes 1572872 | tf_op jit(solution)/shard_map/ppermute | solution.py:298
  19.3 0.1 hop.7.refs_0_
  19.4 1.4 %collective-permute-done.5.incoming_ref = f32[2,256,256]{2,1,0:T(8,128)S(1)} collective-permute-done((f32[2,256,256]{2,1,0:T(8,128)S(1)}, f32[2,256,256]{2,1,0:T(8,128)S(1)}, u32[]{:S(2)}, u32[]{:S(2)}) %collective-permute-start.5) | collective-permute-done | bytes 524320 | tf_op jit(solution)/shard_map/ppermute | solution.py:298
  20.8 0.1 last.1
  20.9 0.0 copy-start.3
  20.9 1.6 %collective-permute-start.10 = (bf16[2,32,512]{2,1,0:T(8,128)(2,1)S(1)}, bf16[2,32,512]{2,1,0:T(8,128)(2,1)S(1)}, u32[]{:S(2)}, u32[]{:S(2)}) collective-permute-start(bf16[2,32,512]{2,1,0:T(8,128)(2,1)S(1)} %get-tuple-element.46), channel_id=1, source_target_pairs={{0,8},{4,12},{8,0},{12,4},{16,24},{20,28},{24,16},{28,20},{1,9},{5... | collective-permute-start | bytes 196616 | tf_op jit(solution)/shard_map/ppermute | solution.py:326
  22.5 1.4 %collective-permute-start.11 = (bf16[2,32,512]{2,1,0:T(8,128)(2,1)S(1)}, bf16[2,32,512]{2,1,0:T(8,128)(2,1)S(1)}, u32[]{:S(2)}, u32[]{:S(2)}) collective-permute-start(bf16[2,32,512]{2,1,0:T(8,128)(2,1)S(1)} %get-tuple-element.47), channel_id=1, source_target_pairs={{0,12},{4,8},{8,4},{12,0},{16,28},{20,24},{24,20},{28,16},{1,13},{... | collective-permute-start | bytes 196616 | tf_op jit(solution)/shard_map/ppermute | solution.py:326
  23.9 0.5 collective-permute-start.12
  24.4 2.6 %collective-permute-start.6 = (bf16[2,32,512]{2,1,0:T(8,128)(2,1)S(1)}, bf16[2,32,512]{2,1,0:T(8,128)(2,1)S(1)}, u32[]{:S(2)}, u32[]{:S(2)}) collective-permute-start(bf16[2,32,512]{2,1,0:T(8,128)(2,1)S(1)} %get-tuple-element.42), channel_id=1, source_target_pairs={{0,16},{4,20},{8,24},{12,28},{16,0},{20,4},{24,8},{28,12},{1,17},{... | collective-permute-start | bytes 196616 | tf_op jit(solution)/shard_map/ppermute | solution.py:326
  27.0 1.3 %collective-permute-start.7 = (bf16[2,32,512]{2,1,0:T(8,128)(2,1)S(1)}, bf16[2,32,512]{2,1,0:T(8,128)(2,1)S(1)}, u32[]{:S(2)}, u32[]{:S(2)}) collective-permute-start(bf16[2,32,512]{2,1,0:T(8,128)(2,1)S(1)} %get-tuple-element.43), channel_id=1, source_target_pairs={{0,20},{4,16},{8,28},{12,24},{16,4},{20,0},{24,12},{28,8},{1,21},{... | collective-permute-start | bytes 196616 | tf_op jit(solution)/shard_map/ppermute | solution.py:326
  28.3 3.6 %collective-permute-start.8 = (bf16[2,32,512]{2,1,0:T(8,128)(2,1)S(1)}, bf16[2,32,512]{2,1,0:T(8,128)(2,1)S(1)}, u32[]{:S(2)}, u32[]{:S(2)}) collective-permute-start(bf16[2,32,512]{2,1,0:T(8,128)(2,1)S(1)} %get-tuple-element.44), channel_id=1, source_target_pairs={{0,24},{4,28},{8,16},{12,20},{16,8},{20,12},{24,0},{28,4},{1,25},{... | collective-permute-start | bytes 196616 | tf_op jit(solution)/shard_map/ppermute | solution.py:326
  31.9 0.2 collective-permute-start.9
  32.1 0.1 copy.16
  32.2 0.0 copy-start
  32.2 0.1 copy.17.refs_0_
  32.3 0.6 copy-done
  32.9 0.0 copy-done.1
  32.9 0.0 copy-done.2
  33.0 4.3 %collective-permute-done.7.refs_5_ = bf16[2,32,512]{2,1,0:T(8,128)(2,1)S(1)} collective-permute-done((bf16[2,32,512]{2,1,0:T(8,128)(2,1)S(1)}, bf16[2,32,512]{2,1,0:T(8,128)(2,1)S(1)}, u32[]{:S(2)}, u32[]{:S(2)}) %collective-permute-start.7) | collective-permute-done | bytes 65568 | tf_op jit(solution)/shard_map/ppermute | solution.py:326
  37.2 1.7 %collective-permute-done.9.refs_7_ = bf16[2,32,512]{2,1,0:T(8,128)(2,1)S(1)} collective-permute-done((bf16[2,32,512]{2,1,0:T(8,128)(2,1)S(1)}, bf16[2,32,512]{2,1,0:T(8,128)(2,1)S(1)}, u32[]{:S(2)}, u32[]{:S(2)}) %collective-permute-start.9) | collective-permute-done | bytes 65568 | tf_op jit(solution)/shard_map/ppermute | solution.py:326
  39.0 1.3 %energy.6 = (bf16[2,32,512]{2,1,0:T(8,128)(2,1)S(1)}, bf16[2,32,512]{2,1,0:T(8,128)(2,1)S(1)}, bf16[2,32,512]{2,1,0:T(8,128)(2,1)S(1)}) custom-call(s32[1]{0:T(128)} %bitcast.1.me_ref, s32[8,24]{1,0:T(8,128)S(1)} %get-tuple-element.38.refs_0_, s32[1,8]{1,0:T(1,128)S(1)} %get-tuple-element.39.refs_1_, s32[8,8]{1,0:T(8,128)S(1)} %get-tuple-element.40.refs_2_, ...), custom_call_target="tpu_custom_call" | custom-call | flops 39321600 | bytes 524288 | tf_op jit(solution)/shard_map/energy/pallas_call | solution.py:345
  40.3 2.1 %collective-permute-start.17 = (bf16[2,32,512]{2,1,0:T(8,128)(2,1)S(1)}, bf16[2,32,512]{2,1,0:T(8,128)(2,1)S(1)}, u32[]{:S(2)}, u32[]{:S(2)}) collective-permute-start(bf16[2,32,512]{2,1,0:T(8,128)(2,1)S(1)} %get-tuple-element.53), channel_id=1, source_target_pairs={{0,8},{4,12},{8,0},{12,4},{16,24},{20,28},{24,16},{28,20},{1,9},{5... | collective-permute-start | bytes 196616 | tf_op jit(solution)/shard_map/ppermute | solution.py:326
  42.4 0.7 %collective-permute-start.18 = (bf16[2,32,512]{2,1,0:T(8,128)(2,1)S(1)}, bf16[2,32,512]{2,1,0:T(8,128)(2,1)S(1)}, u32[]{:S(2)}, u32[]{:S(2)}) collective-permute-start(bf16[2,32,512]{2,1,0:T(8,128)(2,1)S(1)} %get-tuple-element.54), channel_id=1, source_target_pairs={{0,12},{4,8},{8,4},{12,0},{16,28},{20,24},{24,20},{28,16},{1,13},{... | collective-permute-start | bytes 196616 | tf_op jit(solution)/shard_map/ppermute | solution.py:326
  43.1 0.9 %collective-permute-start.19 = (bf16[2,32,512]{2,1,0:T(8,128)(2,1)S(1)}, bf16[2,32,512]{2,1,0:T(8,128)(2,1)S(1)}, u32[]{:S(2)}, u32[]{:S(2)}) collective-permute-start(bf16[2,32,512]{2,1,0:T(8,128)(2,1)S(1)} %get-tuple-element.55), channel_id=1, source_target_pairs={{0,4},{4,0},{8,12},{12,8},{16,20},{20,16},{24,28},{28,24},{1,5},{5... | collective-permute-start | bytes 196616 | tf_op jit(solution)/shard_map/ppermute | solution.py:326
  44.0 1.8 %energy.5 = (bf16[2,32,512]{2,1,0:T(8,128)(2,1)S(1)}, bf16[2,32,512]{2,1,0:T(8,128)(2,1)S(1)}, bf16[2,32,512]{2,1,0:T(8,128)(2,1)S(1)}) custom-call(s32[1]{0:T(128)} %bitcast.1.me_ref, s32[8,24]{1,0:T(8,128)S(1)} %get-tuple-element.38.refs_0_, s32[1,8]{1,0:T(1,128)S(1)} %get-tuple-element.39.refs_1_, s32[8,8]{1,0:T(8,128)S(1)} %get-tuple-element.40.refs_2_, ...), custom_call_target="tpu_custom_call" | custom-call | flops 39321600 | bytes 524288 | tf_op jit(solution)/shard_map/energy/pallas_call | solution.py:345
  45.8 3.7 %collective-permute-start.14 = (bf16[2,32,512]{2,1,0:T(8,128)(2,1)S(1)}, bf16[2,32,512]{2,1,0:T(8,128)(2,1)S(1)}, u32[]{:S(2)}, u32[]{:S(2)}) collective-permute-start(bf16[2,32,512]{2,1,0:T(8,128)(2,1)S(1)} %get-tuple-element.50), channel_id=1, source_target_pairs={{0,20},{4,16},{8,28},{12,24},{16,4},{20,0},{24,12},{28,8},{1,21},{... | collective-permute-start | bytes 196616 | tf_op jit(solution)/shard_map/ppermute | solution.py:326
  49.5 1.1 %collective-permute-start.15 = (bf16[2,32,512]{2,1,0:T(8,128)(2,1)S(1)}, bf16[2,32,512]{2,1,0:T(8,128)(2,1)S(1)}, u32[]{:S(2)}, u32[]{:S(2)}) collective-permute-start(bf16[2,32,512]{2,1,0:T(8,128)(2,1)S(1)} %get-tuple-element.51), channel_id=1, source_target_pairs={{0,24},{4,28},{8,16},{12,20},{16,8},{20,12},{24,0},{28,4},{1,25},{... | collective-permute-start | bytes 196616 | tf_op jit(solution)/shard_map/ppermute | solution.py:326
  50.6 0.8 %energy.4 = bf16[2,32,512]{2,1,0:T(8,128)(2,1)S(1)} custom-call(s32[1]{0:T(128)} %bitcast.1.me_ref, s32[8,24]{1,0:T(8,128)S(1)} %get-tuple-element.38.refs_0_, s32[1,8]{1,0:T(1,128)S(1)} %get-tuple-element.39.refs_1_, s32[8,8]{1,0:T(8,128)S(1)} %get-tuple-element.40.refs_2_, f32[1,16]{1,0:T(1,128)S(1)} %get-tuple-element.41.refs_3_, ...), custom_call_target="tpu_custom_call" | custom-call | flops 13107200 | bytes 524288 | tf_op jit(solution)/shard_map/energy/pallas_call | solution.py:345
  51.4 3.8 %collective-permute-start.16 = (bf16[2,32,512]{2,1,0:T(8,128)(2,1)S(1)}, bf16[2,32,512]{2,1,0:T(8,128)(2,1)S(1)}, u32[]{:S(2)}, u32[]{:S(2)}) collective-permute-start(bf16[2,32,512]{2,1,0:T(8,128)(2,1)S(1)} %get-tuple-element.52), channel_id=1, source_target_pairs={{0,28},{4,24},{8,20},{12,16},{16,12},{20,8},{24,4},{28,0},{1,29},{... | collective-permute-start | bytes 196616 | tf_op jit(solution)/shard_map/ppermute | solution.py:326
  55.2 0.8 %emit.1 = bf16[2,1,256,512]{3,2,1,0:T(8,128)(2,1)} custom-call(f32[2,256,256]{2,1,0:T(8,128)S(1)} %hop.7.refs_0_, f32[2,256,256]{2,1,0:T(8,128)S(1)} %get-tuple-element.37.refs_1_), custom_call_target="tpu_custom_call" | custom-call | flops 131072 | bytes 1572864 | tf_op jit(solution)/shard_map/emit/pallas_call | solution.py:315
  56.1 1.1 %energy.7.refs_7_ = bf16[2,32,512]{2,1,0:T(8,128)(2,1)S(1)} custom-call(s32[1]{0:T(128)} %bitcast.1.me_ref, s32[8,24]{1,0:T(8,128)S(1)} %get-tuple-element.38.refs_0_, s32[1,8]{1,0:T(1,128)S(1)} %get-tuple-element.39.refs_1_, s32[8,8]{1,0:T(8,128)S(1)} %get-tuple-element.40.refs_2_, f32[1,16]{1,0:T(1,128)S(1)} %get-tuple-element.41.refs_3_, ...), custom_call_target="tpu_custom_call" | custom-call | flops 13107200 | bytes 524288 | tf_op jit(solution)/shard_map/energy/pallas_call | solution.py:345
  57.2 1.3 %collective-permute-done.16.refs_3_ = bf16[2,32,512]{2,1,0:T(8,128)(2,1)S(1)} collective-permute-done((bf16[2,32,512]{2,1,0:T(8,128)(2,1)S(1)}, bf16[2,32,512]{2,1,0:T(8,128)(2,1)S(1)}, u32[]{:S(2)}, u32[]{:S(2)}) %collective-permute-start.16) | collective-permute-done | bytes 65568 | tf_op jit(solution)/shard_map/ppermute | solution.py:326
  58.5 2.2 %collective-permute-done.13.refs_0_ = bf16[2,32,512]{2,1,0:T(8,128)(2,1)S(1)} collective-permute-done((bf16[2,32,512]{2,1,0:T(8,128)(2,1)S(1)}, bf16[2,32,512]{2,1,0:T(8,128)(2,1)S(1)}, u32[]{:S(2)}, u32[]{:S(2)}) %collective-permute-start.13) | collective-permute-done | bytes 65568 | tf_op jit(solution)/shard_map/ppermute | solution.py:326
  60.8 1.0 %gather.1 = f32[2,1,256,512]{3,2,1,0:T(8,128)} custom-call(s32[1]{0:T(128)} %bitcast.1.me_ref, bf16[2,32,512]{2,1,0:T(8,128)(2,1)S(1)} %collective-permute-done.13.refs_0_, bf16[2,32,512]{2,1,0:T(8,128)(2,1)S(1)} %collective-permute-done.14.refs_1_, bf16[2,32,512]{2,1,0:T(8,128)(2,1)S(1)} %collective-permute-done.15.refs_2_, ...), custom_call_target="tpu_custom_call" | custom-call | flops 131072 | bytes 1572864 | tf_op jit(solution)/shard_map/gather/pallas_call | solution.py:369
  (19 shorter events, 0.1 us)
Async XLA Ops:
  2.5 3.4 %collective-permute-start = (f32[2,256,256]{2,1,0:T(8,128)S(1)}, f32[2,256,256]{2,1,0:T(8,128)}, u32[]{:S(2)}, u32[]{:S(2)}) collective-permute-start(f32[2,256,256]{2,1,0:T(8,128)S(1)} %get-tuple-element.31.state_ref), channel_id=1, source_target_pairs={{0,1},{4,5},{8,9},{12,13},{16,17},{20,21},{24,25},{28,29}} | collective-permute-start | bytes 1572872 | tf_op jit(solution)/shard_map/ppermute | solution.py:298
  4.5 3.7 %collective-permute-start.3 = (f32[2,256,256]{2,1,0:T(8,128)S(1)}, f32[2,256,256]{2,1,0:T(8,128)S(1)}, u32[]{:S(2)}, u32[]{:S(2)}) collective-permute-start(f32[2,256,256]{2,1,0:T(8,128)S(1)} %drive.1.state_ref), channel_id=1, source_target_pairs={{0,1},{4,5},{8,9},{12,13},{16,17},{20,21},{24,25},{28,29}} | collective-permute-start | bytes 1572872 | tf_op jit(solution)/shard_map/ppermute | solution.py:298
  7.0 7.7 %collective-permute-start.1 = (bf16[2,256,256]{2,1,0:T(8,128)(2,1)S(1)}, bf16[2,256,256]{2,1,0:T(8,128)(2,1)S(1)}, u32[]{:S(2)}, u32[]{:S(2)}) collective-permute-start(bf16[2,256,256]{2,1,0:T(8,128)(2,1)S(1)} %get-tuple-element.33), channel_id=1, source_target_pairs={{1,2},{5,6},{9,10},{13,14},{17,18},{21,22},{25,26},{29,30}} | collective-permute-start | bytes 786440 | tf_op jit(solution)/shard_map/ppermute | solution.py:298
  8.4 9.1 %collective-permute-start.4 = (bf16[2,256,256]{2,1,0:T(8,128)(2,1)S(1)}, bf16[2,256,256]{2,1,0:T(8,128)(2,1)S(1)}, u32[]{:S(2)}, u32[]{:S(2)}) collective-permute-start(bf16[2,256,256]{2,1,0:T(8,128)(2,1)S(1)} %get-tuple-element.36), channel_id=1, source_target_pairs={{1,2},{5,6},{9,10},{13,14},{17,18},{21,22},{25,26},{29,30}} | collective-permute-start | bytes 786440 | tf_op jit(solution)/shard_map/ppermute | solution.py:298
  15.1 4.1 %collective-permute-start.2 = (f32[2,256,256]{2,1,0:T(8,128)S(1)}, f32[2,256,256]{2,1,0:T(8,128)S(1)}, u32[]{:S(2)}, u32[]{:S(2)}) collective-permute-start(f32[2,256,256]{2,1,0:T(8,128)S(1)} %hop.6.state_ref), channel_id=1, source_target_pairs={{2,3},{6,7},{10,11},{14,15},{18,19},{22,23},{26,27},{30,31}} | collective-permute-start | bytes 1572872 | tf_op jit(solution)/shard_map/ppermute | solution.py:298
  17.9 2.8 %collective-permute-start.5 = (f32[2,256,256]{2,1,0:T(8,128)S(1)}, f32[2,256,256]{2,1,0:T(8,128)S(1)}, u32[]{:S(2)}, u32[]{:S(2)}) collective-permute-start(f32[2,256,256]{2,1,0:T(8,128)S(1)} %hop.9.state_ref), channel_id=1, source_target_pairs={{2,3},{6,7},{10,11},{14,15},{18,19},{22,23},{26,27},{30,31}} | collective-permute-start | bytes 1572872 | tf_op jit(solution)/shard_map/ppermute | solution.py:298
  20.9 11.2 %copy-start.3 = (s32[8,8,3]{1,0,2:T(8,128)S(1)}, s32[8,8,3]{1,0,2:T(8,128)}, u32[]{:S(2)}) copy-start(s32[8,8,3]{1,0,2:T(8,128)} %param.10) | copy-start | bytes 2308
  20.9 7.4 %collective-permute-start.10 = (bf16[2,32,512]{2,1,0:T(8,128)(2,1)S(1)}, bf16[2,32,512]{2,1,0:T(8,128)(2,1)S(1)}, u32[]{:S(2)}, u32[]{:S(2)}) collective-permute-start(bf16[2,32,512]{2,1,0:T(8,128)(2,1)S(1)} %get-tuple-element.46), channel_id=1, source_target_pairs={{0,8},{4,12},{8,0},{12,4},{16,24},{20,28},{24,16},{28,20},{1,9},{5... | collective-permute-start | bytes 196616 | tf_op jit(solution)/shard_map/ppermute | solution.py:326
  22.5 9.4 %collective-permute-start.11 = (bf16[2,32,512]{2,1,0:T(8,128)(2,1)S(1)}, bf16[2,32,512]{2,1,0:T(8,128)(2,1)S(1)}, u32[]{:S(2)}, u32[]{:S(2)}) collective-permute-start(bf16[2,32,512]{2,1,0:T(8,128)(2,1)S(1)} %get-tuple-element.47), channel_id=1, source_target_pairs={{0,12},{4,8},{8,4},{12,0},{16,28},{20,24},{24,20},{28,16},{1,13},{... | collective-permute-start | bytes 196616 | tf_op jit(solution)/shard_map/ppermute | solution.py:326
  23.9 9.0 %collective-permute-start.12 = (bf16[2,32,512]{2,1,0:T(8,128)(2,1)S(1)}, bf16[2,32,512]{2,1,0:T(8,128)(2,1)S(1)}, u32[]{:S(2)}, u32[]{:S(2)}) collective-permute-start(bf16[2,32,512]{2,1,0:T(8,128)(2,1)S(1)} %get-tuple-element.48), channel_id=1, source_target_pairs={{0,4},{4,0},{8,12},{12,8},{16,20},{20,16},{24,28},{28,24},{1,5},{5... | collective-permute-start | bytes 196616 | tf_op jit(solution)/shard_map/ppermute | solution.py:326
  24.4 8.5 %collective-permute-start.6 = (bf16[2,32,512]{2,1,0:T(8,128)(2,1)S(1)}, bf16[2,32,512]{2,1,0:T(8,128)(2,1)S(1)}, u32[]{:S(2)}, u32[]{:S(2)}) collective-permute-start(bf16[2,32,512]{2,1,0:T(8,128)(2,1)S(1)} %get-tuple-element.42), channel_id=1, source_target_pairs={{0,16},{4,20},{8,24},{12,28},{16,0},{20,4},{24,8},{28,12},{1,17},{... | collective-permute-start | bytes 196616 | tf_op jit(solution)/shard_map/ppermute | solution.py:326
  27.0 10.2 %collective-permute-start.7 = (bf16[2,32,512]{2,1,0:T(8,128)(2,1)S(1)}, bf16[2,32,512]{2,1,0:T(8,128)(2,1)S(1)}, u32[]{:S(2)}, u32[]{:S(2)}) collective-permute-start(bf16[2,32,512]{2,1,0:T(8,128)(2,1)S(1)} %get-tuple-element.43), channel_id=1, source_target_pairs={{0,20},{4,16},{8,28},{12,24},{16,4},{20,0},{24,12},{28,8},{1,21},{... | collective-permute-start | bytes 196616 | tf_op jit(solution)/shard_map/ppermute | solution.py:326
  28.3 8.9 %collective-permute-start.8 = (bf16[2,32,512]{2,1,0:T(8,128)(2,1)S(1)}, bf16[2,32,512]{2,1,0:T(8,128)(2,1)S(1)}, u32[]{:S(2)}, u32[]{:S(2)}) collective-permute-start(bf16[2,32,512]{2,1,0:T(8,128)(2,1)S(1)} %get-tuple-element.44), channel_id=1, source_target_pairs={{0,24},{4,28},{8,16},{12,20},{16,8},{20,12},{24,0},{28,4},{1,25},{... | collective-permute-start | bytes 196616 | tf_op jit(solution)/shard_map/ppermute | solution.py:326
  31.9 7.1 %collective-permute-start.9 = (bf16[2,32,512]{2,1,0:T(8,128)(2,1)S(1)}, bf16[2,32,512]{2,1,0:T(8,128)(2,1)S(1)}, u32[]{:S(2)}, u32[]{:S(2)}) collective-permute-start(bf16[2,32,512]{2,1,0:T(8,128)(2,1)S(1)} %get-tuple-element.45), channel_id=1, source_target_pairs={{0,28},{4,24},{8,20},{12,16},{16,12},{20,8},{24,4},{28,0},{1,29},{... | collective-permute-start | bytes 196616 | tf_op jit(solution)/shard_map/ppermute | solution.py:326
  32.2 0.7 %copy-start = (s32[8,8]{1,0:T(8,128)S(1)}, s32[8,8]{1,0:T(8,128)}, u32[]{:S(2)}) copy-start(s32[8,8]{1,0:T(8,128)} %refs_2_.1) | copy-start | bytes 772
  32.3 0.7 %copy-start.1 = (s32[8]{0:T(128)S(1)}, s32[8]{0:T(128)}, u32[]{:S(2)}) copy-start(s32[8]{0:T(128)} %param.11) | copy-start | bytes 100
  32.3 0.7 %copy-start.2 = (f32[16]{0:T(128)S(1)}, f32[16]{0:T(128)}, u32[]{:S(2)}) copy-start(f32[16]{0:T(128)} %param.13) | copy-start | bytes 196
  40.3 11.1 %collective-permute-start.17 = (bf16[2,32,512]{2,1,0:T(8,128)(2,1)S(1)}, bf16[2,32,512]{2,1,0:T(8,128)(2,1)S(1)}, u32[]{:S(2)}, u32[]{:S(2)}) collective-permute-start(bf16[2,32,512]{2,1,0:T(8,128)(2,1)S(1)} %get-tuple-element.53), channel_id=1, source_target_pairs={{0,8},{4,12},{8,0},{12,4},{16,24},{20,28},{24,16},{28,20},{1,9},{5... | collective-permute-start | bytes 196616 | tf_op jit(solution)/shard_map/ppermute | solution.py:326
  42.4 12.8 %collective-permute-start.18 = (bf16[2,32,512]{2,1,0:T(8,128)(2,1)S(1)}, bf16[2,32,512]{2,1,0:T(8,128)(2,1)S(1)}, u32[]{:S(2)}, u32[]{:S(2)}) collective-permute-start(bf16[2,32,512]{2,1,0:T(8,128)(2,1)S(1)} %get-tuple-element.54), channel_id=1, source_target_pairs={{0,12},{4,8},{8,4},{12,0},{16,28},{20,24},{24,20},{28,16},{1,13},{... | collective-permute-start | bytes 196616 | tf_op jit(solution)/shard_map/ppermute | solution.py:326
  43.1 14.1 %collective-permute-start.19 = (bf16[2,32,512]{2,1,0:T(8,128)(2,1)S(1)}, bf16[2,32,512]{2,1,0:T(8,128)(2,1)S(1)}, u32[]{:S(2)}, u32[]{:S(2)}) collective-permute-start(bf16[2,32,512]{2,1,0:T(8,128)(2,1)S(1)} %get-tuple-element.55), channel_id=1, source_target_pairs={{0,4},{4,0},{8,12},{12,8},{16,20},{20,16},{24,28},{28,24},{1,5},{5... | collective-permute-start | bytes 196616 | tf_op jit(solution)/shard_map/ppermute | solution.py:326
  45.8 11.5 %collective-permute-start.14 = (bf16[2,32,512]{2,1,0:T(8,128)(2,1)S(1)}, bf16[2,32,512]{2,1,0:T(8,128)(2,1)S(1)}, u32[]{:S(2)}, u32[]{:S(2)}) collective-permute-start(bf16[2,32,512]{2,1,0:T(8,128)(2,1)S(1)} %get-tuple-element.50), channel_id=1, source_target_pairs={{0,20},{4,16},{8,28},{12,24},{16,4},{20,0},{24,12},{28,8},{1,21},{... | collective-permute-start | bytes 196616 | tf_op jit(solution)/shard_map/ppermute | solution.py:326
  49.5 7.7 %collective-permute-start.15 = (bf16[2,32,512]{2,1,0:T(8,128)(2,1)S(1)}, bf16[2,32,512]{2,1,0:T(8,128)(2,1)S(1)}, u32[]{:S(2)}, u32[]{:S(2)}) collective-permute-start(bf16[2,32,512]{2,1,0:T(8,128)(2,1)S(1)} %get-tuple-element.51), channel_id=1, source_target_pairs={{0,24},{4,28},{8,16},{12,20},{16,8},{20,12},{24,0},{28,4},{1,25},{... | collective-permute-start | bytes 196616 | tf_op jit(solution)/shard_map/ppermute | solution.py:326
  51.4 7.1 %collective-permute-start.16 = (bf16[2,32,512]{2,1,0:T(8,128)(2,1)S(1)}, bf16[2,32,512]{2,1,0:T(8,128)(2,1)S(1)}, u32[]{:S(2)}, u32[]{:S(2)}) collective-permute-start(bf16[2,32,512]{2,1,0:T(8,128)(2,1)S(1)} %get-tuple-element.52), channel_id=1, source_target_pairs={{0,28},{4,24},{8,20},{12,16},{16,12},{20,8},{24,4},{28,0},{1,29},{... | collective-permute-start | bytes 196616 | tf_op jit(solution)/shard_map/ppermute | solution.py:326
  55.2 5.5 %collective-permute-start.13 = (bf16[2,32,512]{2,1,0:T(8,128)(2,1)S(1)}, bf16[2,32,512]{2,1,0:T(8,128)(2,1)S(1)}, u32[]{:S(2)}, u32[]{:S(2)}) collective-permute-start(bf16[2,32,512]{2,1,0:T(8,128)(2,1)S(1)} %energy.4), channel_id=1, source_target_pairs={{0,16},{4,20},{8,24},{12,28},{16,0},{20,4},{24,8},{28,12},{1,17},{... | collective-permute-start | bytes 196616 | tf_op jit(solution)/shard_map/ppermute | solution.py:326

commit v3 on v2

--- a/solution.py
+++ b/solution.py
@@ -214,6 +214,12 @@
             out_ref[part, 0, pl.ds(start, rows), :] = piece_ref[part].astype(F32)
 
 
+def relay_pairs(times, turn):
+    if turn % 2 == 0:
+        return [(block, block ^ 1) for block in range(times)]
+    return [(block, (block + 1) % times) for block in range(times)]
+
+
 def step_order(moms):
     return sorted(range(1, moms), key=lambda step: (-step.bit_length(), step))
 
@@ -295,7 +301,7 @@
                 kinds = [F32] if turn % 2 == 0 else [F32, BF16]
                 outs = hop(turn, state[chunk], arrived[chunk], kinds)
                 state[chunk], sent[chunk] = outs[0], outs[-1]
-            arrived[chunk] = lax.ppermute(sent[chunk], "tm", [(turn, turn + 1)])
+            arrived[chunk] = lax.ppermute(sent[chunk], "tm", relay_pairs(times, turn))
 
     ready = []
     for chunk in range(chunks - 1):

time: 62.1 us -> 58.2 us (0.937)
  starting transfers between devices: 30.9 us -> 24.3 us
  waiting for transfers between devices: 17 us -> 19.4 us
    ppermute x6, starting transfers between devices: 7.42 us -> 1.05 us  [local(): arrived[chunk] = lax.ppermute(sent[chunk], 'tm', relay_pairs(times, turn))]
    ppermute x6, waiting for transfers between devices: 7.4 us -> 9.85 us  [local(): arrived[chunk] = lax.ppermute(sent[chunk], 'tm', relay_pairs(times, turn))]
  transfers between devices with their start and end apart: 20 -> 20, of which waited for: 7 -> 8; matrix products, arithmetic and copies ran while one was open for 0% -> 0% of each run, Pallas kernels for 13% -> 14%
where the time goes in v3:
time: 58.2 us; the launch traced here: 57.6 us
  starting transfers between devices  24.3 us (42%)
  waiting for transfers between devices  19.4 us (33%)
  Pallas kernels  12.2 us (21%)
  local copies, waits for them, and re-layouts  0.84 us (1%)
  between operations  0.83 us (1%)
    ppermute x14, starting transfers between devices, swap(): return lax.ppermute(value, 'mom', [(at, at ^ step) for at in range(moms)])  23.3 us
    ppermute x6, waiting for transfers between devices, local(): arrived[chunk] = lax.ppermute(sent[chunk], 'tm', relay_pairs(times, turn))  9.85 us
    ppermute x14, waiting for transfers between devices, swap(): return lax.ppermute(value, 'mom', [(at, at ^ step) for at in range(moms)])  9.58 us
    pallas_call x4, Pallas kernels, energy(): pl.pallas_call(functools.partial(energy_kernel, everyone, targets), out_s...  5.05 us
    pallas_call x5, Pallas kernels, hop(): pl.pallas_call(functools.partial(hop_kernel, turn), out_shape=[jax.ShapeD...  2.17 us
    pallas_call x1, Pallas kernels, local(): pl.pallas_call(load_kernel, out_shape=[slabs[0], square, square, *slabs[1...  1.82 us
  transfers between devices with their start and end apart: 20, of which 8 were waited for; matrix products, arithmetic and copies ran while one was open for 0% of the time, Pallas kernels for 14%

profile of v3, /device:TPU:4, one launch (start us, length us, event | category | flops | bytes accessed | tf_op | source)
XLA Modules:
  0.0 57.6 jit_solution(3467631299931104142)
XLA Ops:
  0.6 1.8 %load.1 = (f32[2,256,256]{2,1,0:T(8,128)S(1)}, f32[2,256,256]{2,1,0:T(8,128)S(1)}, f32[2,256,256]{2,1,0:T(8,128)S(1)}, f32[2,256,256]{2,1,0:T(8,128)S(1)}) custom-call(f32[2,1,1,256,256]{4,3,2,1,0:T(8,128)} %inverse_ref.1, f32[2,1,1,256,256]{4,3,2,1,0:T(8,128)} %coupling_ref.1, f32[2,1,256,512]{3,2,1,0:T(8,128)} %source_ref.1), custom_call_target="tpu_custom_call" | custom-call | flops 402653184 | bytes 2097152 | tf_op jit(solution)/shard_map/load/pallas_call | solution.py:243
  2.5 0.1 collective-permute-start
  2.5 0.6 %drive.1.state_ref = f32[2,256,256]{2,1,0:T(8,128)S(1)} custom-call(f32[2,256,256]{2,1,0:T(8,128)S(1)} %get-tuple-element.29.inverse_ref, f32[2,256,256]{2,1,0:T(8,128)S(1)} %get-tuple-element.34.source_ref), custom_call_target="tpu_custom_call" | custom-call | flops 402653184 | bytes 2097152 | tf_op jit(solution)/shard_map/drive/pallas_call | solution.py:269
  3.1 0.6 collective-permute-start.3
  3.7 0.6 %propagator.1.matrix_ref = bf16[2,2,256,256]{3,2,1,0:T(8,128)(2,1)S(1)} custom-call(f32[2,256,256]{2,1,0:T(8,128)S(1)} %get-tuple-element.29.inverse_ref, f32[2,256,256]{2,1,0:T(8,128)S(1)} %get-tuple-element.30.coupling_ref), custom_call_target="tpu_custom_call" | custom-call | flops 402653184 | bytes 2097152 | tf_op jit(solution)/shard_map/propagator/pallas_call | solution.py:257
  4.3 0.3 collective-permute-done.incoming_ref
  4.6 1.1 %hop.5 = (f32[2,256,256]{2,1,0:T(8,128)S(1)}, bf16[2,256,256]{2,1,0:T(8,128)(2,1)S(1)}) custom-call(s32[1]{0:T(128)} %bitcast.at_ref, bf16[2,2,256,256]{3,2,1,0:T(8,128)(2,1)S(1)} %propagator.1.matrix_ref, f32[2,256,256]{2,1,0:T(8,128)S(1)} %get-tuple-element.31.state_ref, ...), custom_call_target="tpu_custom_call", output_to_operand_aliasing={{0}: (2, {})} | custom-call | flops 402653184 | bytes 2097152 | tf_op jit(solution)/shard_map/hop/pallas_call | solution.py:284
  5.7 0.2 collective-permute-start.1
  5.9 0.1 hop.8
  5.9 0.1 collective-permute-start.4
  6.0 5.5 %collective-permute-done.1.incoming_ref = bf16[2,256,256]{2,1,0:T(8,128)(2,1)S(1)} collective-permute-done((bf16[2,256,256]{2,1,0:T(8,128)(2,1)S(1)}, bf16[2,256,256]{2,1,0:T(8,128)(2,1)S(1)}, u32[]{:S(2)}, u32[]{:S(2)}) %collective-permute-start.1) | collective-permute-done | bytes 262176 | tf_op jit(solution)/shard_map/ppermute | solution.py:304
  11.5 0.5 hop.6.state_ref
  12.0 0.1 collective-permute-start.2
  12.1 2.3 %collective-permute-done.4.incoming_ref = bf16[2,256,256]{2,1,0:T(8,128)(2,1)S(1)} collective-permute-done((bf16[2,256,256]{2,1,0:T(8,128)(2,1)S(1)}, bf16[2,256,256]{2,1,0:T(8,128)(2,1)S(1)}, u32[]{:S(2)}, u32[]{:S(2)}) %collective-permute-start.4) | collective-permute-done | bytes 262176 | tf_op jit(solution)/shard_map/ppermute | solution.py:304
  14.3 0.5 hop.9.state_ref
  14.8 0.1 collective-permute-start.5
  14.9 0.1 hop.7.refs_0_
  15.0 1.8 %collective-permute-done.5.incoming_ref = f32[2,256,256]{2,1,0:T(8,128)S(1)} collective-permute-done((f32[2,256,256]{2,1,0:T(8,128)S(1)}, f32[2,256,256]{2,1,0:T(8,128)S(1)}, u32[]{:S(2)}, u32[]{:S(2)}) %collective-permute-start.5) | collective-permute-done | bytes 524320 | tf_op jit(solution)/shard_map/ppermute | solution.py:304
  16.8 0.1 last.1
  16.9 0.0 copy-start.3
  16.9 1.6 %collective-permute-start.10 = (bf16[2,32,512]{2,1,0:T(8,128)(2,1)S(1)}, bf16[2,32,512]{2,1,0:T(8,128)(2,1)S(1)}, u32[]{:S(2)}, u32[]{:S(2)}) collective-permute-start(bf16[2,32,512]{2,1,0:T(8,128)(2,1)S(1)} %get-tuple-element.46), channel_id=1, source_target_pairs={{0,8},{4,12},{8,0},{12,4},{16,24},{20,28},{24,16},{28,20},{1,9},{5... | collective-permute-start | bytes 196616 | tf_op jit(solution)/shard_map/ppermute | solution.py:332
  18.6 1.4 %collective-permute-start.11 = (bf16[2,32,512]{2,1,0:T(8,128)(2,1)S(1)}, bf16[2,32,512]{2,1,0:T(8,128)(2,1)S(1)}, u32[]{:S(2)}, u32[]{:S(2)}) collective-permute-start(bf16[2,32,512]{2,1,0:T(8,128)(2,1)S(1)} %get-tuple-element.47), channel_id=1, source_target_pairs={{0,12},{4,8},{8,4},{12,0},{16,28},{20,24},{24,20},{28,16},{1,13},{... | collective-permute-start | bytes 196616 | tf_op jit(solution)/shard_map/ppermute | solution.py:332
  19.9 0.5 collective-permute-start.12
  20.5 2.6 %collective-permute-start.6 = (bf16[2,32,512]{2,1,0:T(8,128)(2,1)S(1)}, bf16[2,32,512]{2,1,0:T(8,128)(2,1)S(1)}, u32[]{:S(2)}, u32[]{:S(2)}) collective-permute-start(bf16[2,32,512]{2,1,0:T(8,128)(2,1)S(1)} %get-tuple-element.42), channel_id=1, source_target_pairs={{0,16},{4,20},{8,24},{12,28},{16,0},{20,4},{24,8},{28,12},{1,17},{... | collective-permute-start | bytes 196616 | tf_op jit(solution)/shard_map/ppermute | solution.py:332
  23.1 1.3 %collective-permute-start.7 = (bf16[2,32,512]{2,1,0:T(8,128)(2,1)S(1)}, bf16[2,32,512]{2,1,0:T(8,128)(2,1)S(1)}, u32[]{:S(2)}, u32[]{:S(2)}) collective-permute-start(bf16[2,32,512]{2,1,0:T(8,128)(2,1)S(1)} %get-tuple-element.43), channel_id=1, source_target_pairs={{0,20},{4,16},{8,28},{12,24},{16,4},{20,0},{24,12},{28,8},{1,21},{... | collective-permute-start | bytes 196616 | tf_op jit(solution)/shard_map/ppermute | solution.py:332
  24.3 3.6 %collective-permute-start.8 = (bf16[2,32,512]{2,1,0:T(8,128)(2,1)S(1)}, bf16[2,32,512]{2,1,0:T(8,128)(2,1)S(1)}, u32[]{:S(2)}, u32[]{:S(2)}) collective-permute-start(bf16[2,32,512]{2,1,0:T(8,128)(2,1)S(1)} %get-tuple-element.44), channel_id=1, source_target_pairs={{0,24},{4,28},{8,16},{12,20},{16,8},{20,12},{24,0},{28,4},{1,25},{... | collective-permute-start | bytes 196616 | tf_op jit(solution)/shard_map/ppermute | solution.py:332
  27.9 0.2 collective-permute-start.9
  28.1 0.1 copy.16
  28.2 0.1 copy.17.refs_0_
  28.3 0.6 %copy-done = s32[8,8]{1,0:T(8,128)S(1)} copy-done((s32[8,8]{1,0:T(8,128)S(1)}, s32[8,8]{1,0:T(8,128)}, u32[]{:S(2)}) %copy-start) | copy-done | bytes 280
  28.9 0.0 copy-done.1
  29.0 0.0 copy-done.2
  29.0 4.2 %collective-permute-done.7.refs_5_ = bf16[2,32,512]{2,1,0:T(8,128)(2,1)S(1)} collective-permute-done((bf16[2,32,512]{2,1,0:T(8,128)(2,1)S(1)}, bf16[2,32,512]{2,1,0:T(8,128)(2,1)S(1)}, u32[]{:S(2)}, u32[]{:S(2)}) %collective-permute-start.7) | collective-permute-done | bytes 65568 | tf_op jit(solution)/shard_map/ppermute | solution.py:332
  33.2 1.8 %collective-permute-done.9.refs_7_ = bf16[2,32,512]{2,1,0:T(8,128)(2,1)S(1)} collective-permute-done((bf16[2,32,512]{2,1,0:T(8,128)(2,1)S(1)}, bf16[2,32,512]{2,1,0:T(8,128)(2,1)S(1)}, u32[]{:S(2)}, u32[]{:S(2)}) %collective-permute-start.9) | collective-permute-done | bytes 65568 | tf_op jit(solution)/shard_map/ppermute | solution.py:332
  35.0 1.3 %energy.6 = (bf16[2,32,512]{2,1,0:T(8,128)(2,1)S(1)}, bf16[2,32,512]{2,1,0:T(8,128)(2,1)S(1)}, bf16[2,32,512]{2,1,0:T(8,128)(2,1)S(1)}) custom-call(s32[1]{0:T(128)} %bitcast.1.me_ref, s32[8,24]{1,0:T(8,128)S(1)} %get-tuple-element.38.refs_0_, s32[1,8]{1,0:T(1,128)S(1)} %get-tuple-element.39.refs_1_, s32[8,8]{1,0:T(8,128)S(1)} %get-tuple-element.40.refs_2_, ...), custom_call_target="tpu_custom_call" | custom-call | flops 39321600 | bytes 524288 | tf_op jit(solution)/shard_map/energy/pallas_call | solution.py:351
  36.3 2.1 %collective-permute-start.17 = (bf16[2,32,512]{2,1,0:T(8,128)(2,1)S(1)}, bf16[2,32,512]{2,1,0:T(8,128)(2,1)S(1)}, u32[]{:S(2)}, u32[]{:S(2)}) collective-permute-start(bf16[2,32,512]{2,1,0:T(8,128)(2,1)S(1)} %get-tuple-element.53), channel_id=1, source_target_pairs={{0,8},{4,12},{8,0},{12,4},{16,24},{20,28},{24,16},{28,20},{1,9},{5... | collective-permute-start | bytes 196616 | tf_op jit(solution)/shard_map/ppermute | solution.py:332
  38.4 0.5 collective-permute-start.18
  38.9 1.1 %collective-permute-start.19 = (bf16[2,32,512]{2,1,0:T(8,128)(2,1)S(1)}, bf16[2,32,512]{2,1,0:T(8,128)(2,1)S(1)}, u32[]{:S(2)}, u32[]{:S(2)}) collective-permute-start(bf16[2,32,512]{2,1,0:T(8,128)(2,1)S(1)} %get-tuple-element.55), channel_id=1, source_target_pairs={{0,4},{4,0},{8,12},{12,8},{16,20},{20,16},{24,28},{28,24},{1,5},{5... | collective-permute-start | bytes 196616 | tf_op jit(solution)/shard_map/ppermute | solution.py:332
  39.9 1.8 %energy.5 = (bf16[2,32,512]{2,1,0:T(8,128)(2,1)S(1)}, bf16[2,32,512]{2,1,0:T(8,128)(2,1)S(1)}, bf16[2,32,512]{2,1,0:T(8,128)(2,1)S(1)}) custom-call(s32[1]{0:T(128)} %bitcast.1.me_ref, s32[8,24]{1,0:T(8,128)S(1)} %get-tuple-element.38.refs_0_, s32[1,8]{1,0:T(1,128)S(1)} %get-tuple-element.39.refs_1_, s32[8,8]{1,0:T(8,128)S(1)} %get-tuple-element.40.refs_2_, ...), custom_call_target="tpu_custom_call" | custom-call | flops 39321600 | bytes 524288 | tf_op jit(solution)/shard_map/energy/pallas_call | solution.py:351
  41.7 3.5 %collective-permute-start.14 = (bf16[2,32,512]{2,1,0:T(8,128)(2,1)S(1)}, bf16[2,32,512]{2,1,0:T(8,128)(2,1)S(1)}, u32[]{:S(2)}, u32[]{:S(2)}) collective-permute-start(bf16[2,32,512]{2,1,0:T(8,128)(2,1)S(1)} %get-tuple-element.50), channel_id=1, source_target_pairs={{0,20},{4,16},{8,28},{12,24},{16,4},{20,0},{24,12},{28,8},{1,21},{... | collective-permute-start | bytes 196616 | tf_op jit(solution)/shard_map/ppermute | solution.py:332
  45.3 1.0 %collective-permute-start.15 = (bf16[2,32,512]{2,1,0:T(8,128)(2,1)S(1)}, bf16[2,32,512]{2,1,0:T(8,128)(2,1)S(1)}, u32[]{:S(2)}, u32[]{:S(2)}) collective-permute-start(bf16[2,32,512]{2,1,0:T(8,128)(2,1)S(1)} %get-tuple-element.51), channel_id=1, source_target_pairs={{0,24},{4,28},{8,16},{12,20},{16,8},{20,12},{24,0},{28,4},{1,25},{... | collective-permute-start | bytes 196616 | tf_op jit(solution)/shard_map/ppermute | solution.py:332
  46.3 0.8 %energy.4 = bf16[2,32,512]{2,1,0:T(8,128)(2,1)S(1)} custom-call(s32[1]{0:T(128)} %bitcast.1.me_ref, s32[8,24]{1,0:T(8,128)S(1)} %get-tuple-element.38.refs_0_, s32[1,8]{1,0:T(1,128)S(1)} %get-tuple-element.39.refs_1_, s32[8,8]{1,0:T(8,128)S(1)} %get-tuple-element.40.refs_2_, f32[1,16]{1,0:T(1,128)S(1)} %get-tuple-element.41.refs_3_, ...), custom_call_target="tpu_custom_call" | custom-call | flops 13107200 | bytes 524288 | tf_op jit(solution)/shard_map/energy/pallas_call | solution.py:351
  47.2 3.9 %collective-permute-start.16 = (bf16[2,32,512]{2,1,0:T(8,128)(2,1)S(1)}, bf16[2,32,512]{2,1,0:T(8,128)(2,1)S(1)}, u32[]{:S(2)}, u32[]{:S(2)}) collective-permute-start(bf16[2,32,512]{2,1,0:T(8,128)(2,1)S(1)} %get-tuple-element.52), channel_id=1, source_target_pairs={{0,28},{4,24},{8,20},{12,16},{16,12},{20,8},{24,4},{28,0},{1,29},{... | collective-permute-start | bytes 196616 | tf_op jit(solution)/shard_map/ppermute | solution.py:332
  51.0 0.8 %emit.1 = bf16[2,1,256,512]{3,2,1,0:T(8,128)(2,1)} custom-call(f32[2,256,256]{2,1,0:T(8,128)S(1)} %hop.7.refs_0_, f32[2,256,256]{2,1,0:T(8,128)S(1)} %get-tuple-element.37.refs_1_), custom_call_target="tpu_custom_call" | custom-call | flops 131072 | bytes 1572864 | tf_op jit(solution)/shard_map/emit/pallas_call | solution.py:321
  51.9 1.1 %energy.7.refs_7_ = bf16[2,32,512]{2,1,0:T(8,128)(2,1)S(1)} custom-call(s32[1]{0:T(128)} %bitcast.1.me_ref, s32[8,24]{1,0:T(8,128)S(1)} %get-tuple-element.38.refs_0_, s32[1,8]{1,0:T(1,128)S(1)} %get-tuple-element.39.refs_1_, s32[8,8]{1,0:T(8,128)S(1)} %get-tuple-element.40.refs_2_, f32[1,16]{1,0:T(1,128)S(1)} %get-tuple-element.41.refs_3_, ...), custom_call_target="tpu_custom_call" | custom-call | flops 13107200 | bytes 524288 | tf_op jit(solution)/shard_map/energy/pallas_call | solution.py:351
  53.0 1.3 %collective-permute-done.16.refs_3_ = bf16[2,32,512]{2,1,0:T(8,128)(2,1)S(1)} collective-permute-done((bf16[2,32,512]{2,1,0:T(8,128)(2,1)S(1)}, bf16[2,32,512]{2,1,0:T(8,128)(2,1)S(1)}, u32[]{:S(2)}, u32[]{:S(2)}) %collective-permute-start.16) | collective-permute-done | bytes 65568 | tf_op jit(solution)/shard_map/ppermute | solution.py:332
  54.3 2.3 %collective-permute-done.13.refs_0_ = bf16[2,32,512]{2,1,0:T(8,128)(2,1)S(1)} collective-permute-done((bf16[2,32,512]{2,1,0:T(8,128)(2,1)S(1)}, bf16[2,32,512]{2,1,0:T(8,128)(2,1)S(1)}, u32[]{:S(2)}, u32[]{:S(2)}) %collective-permute-start.13) | collective-permute-done | bytes 65568 | tf_op jit(solution)/shard_map/ppermute | solution.py:332
  56.6 1.0 %gather.1 = f32[2,1,256,512]{3,2,1,0:T(8,128)} custom-call(s32[1]{0:T(128)} %bitcast.1.me_ref, bf16[2,32,512]{2,1,0:T(8,128)(2,1)S(1)} %collective-permute-done.13.refs_0_, bf16[2,32,512]{2,1,0:T(8,128)(2,1)S(1)} %collective-permute-done.14.refs_1_, bf16[2,32,512]{2,1,0:T(8,128)(2,1)S(1)} %collective-permute-done.15.refs_2_, ...), custom_call_target="tpu_custom_call" | custom-call | flops 131072 | bytes 1572864 | tf_op jit(solution)/shard_map/gather/pallas_call | solution.py:375
  (19 shorter events, 0.1 us)
Async XLA Ops:
  2.5 2.1 %collective-permute-start = (f32[2,256,256]{2,1,0:T(8,128)S(1)}, f32[2,256,256]{2,1,0:T(8,128)}, u32[]{:S(2)}, u32[]{:S(2)}) collective-permute-start(f32[2,256,256]{2,1,0:T(8,128)S(1)} %get-tuple-element.31.state_ref), channel_id=1, source_target_pairs={{0,1},{1,0},{2,3},{3,2},{4,5},{5,4},{6,7},{7,6},{8,9},{9,8},{10,11... | collective-permute-start | bytes 1572872 | tf_op jit(solution)/shard_map/ppermute | solution.py:304
  3.1 2.7 %collective-permute-start.3 = (f32[2,256,256]{2,1,0:T(8,128)S(1)}, f32[2,256,256]{2,1,0:T(8,128)S(1)}, u32[]{:S(2)}, u32[]{:S(2)}) collective-permute-start(f32[2,256,256]{2,1,0:T(8,128)S(1)} %drive.1.state_ref), channel_id=1, source_target_pairs={{0,1},{1,0},{2,3},{3,2},{4,5},{5,4},{6,7},{7,6},{8,9},{9,8},{10,11... | collective-permute-start | bytes 1572872 | tf_op jit(solution)/shard_map/ppermute | solution.py:304
  5.7 5.8 %collective-permute-start.1 = (bf16[2,256,256]{2,1,0:T(8,128)(2,1)S(1)}, bf16[2,256,256]{2,1,0:T(8,128)(2,1)S(1)}, u32[]{:S(2)}, u32[]{:S(2)}) collective-permute-start(bf16[2,256,256]{2,1,0:T(8,128)(2,1)S(1)} %get-tuple-element.33), channel_id=1, source_target_pairs={{0,1},{1,2},{2,3},{3,0},{4,5},{5,6},{6,7},{7,4},{8,9},{9,10},{10,1... | collective-permute-start | bytes 786440 | tf_op jit(solution)/shard_map/ppermute | solution.py:304
  5.9 8.4 %collective-permute-start.4 = (bf16[2,256,256]{2,1,0:T(8,128)(2,1)S(1)}, bf16[2,256,256]{2,1,0:T(8,128)(2,1)S(1)}, u32[]{:S(2)}, u32[]{:S(2)}) collective-permute-start(bf16[2,256,256]{2,1,0:T(8,128)(2,1)S(1)} %get-tuple-element.36), channel_id=1, source_target_pairs={{0,1},{1,2},{2,3},{3,0},{4,5},{5,6},{6,7},{7,4},{8,9},{9,10},{10,1... | collective-permute-start | bytes 786440 | tf_op jit(solution)/shard_map/ppermute | solution.py:304
  12.0 2.9 %collective-permute-start.2 = (f32[2,256,256]{2,1,0:T(8,128)S(1)}, f32[2,256,256]{2,1,0:T(8,128)S(1)}, u32[]{:S(2)}, u32[]{:S(2)}) collective-permute-start(f32[2,256,256]{2,1,0:T(8,128)S(1)} %hop.6.state_ref), channel_id=1, source_target_pairs={{0,1},{1,0},{2,3},{3,2},{4,5},{5,4},{6,7},{7,6},{8,9},{9,8},{10,11... | collective-permute-start | bytes 1572872 | tf_op jit(solution)/shard_map/ppermute | solution.py:304
  14.8 2.0 %collective-permute-start.5 = (f32[2,256,256]{2,1,0:T(8,128)S(1)}, f32[2,256,256]{2,1,0:T(8,128)S(1)}, u32[]{:S(2)}, u32[]{:S(2)}) collective-permute-start(f32[2,256,256]{2,1,0:T(8,128)S(1)} %hop.9.state_ref), channel_id=1, source_target_pairs={{0,1},{1,0},{2,3},{3,2},{4,5},{5,4},{6,7},{7,6},{8,9},{9,8},{10,11... | collective-permute-start | bytes 1572872 | tf_op jit(solution)/shard_map/ppermute | solution.py:304
  16.9 11.2 %copy-start.3 = (s32[8,8,3]{1,0,2:T(8,128)S(1)}, s32[8,8,3]{1,0,2:T(8,128)}, u32[]{:S(2)}) copy-start(s32[8,8,3]{1,0,2:T(8,128)} %param.10) | copy-start | bytes 2308
  16.9 7.4 %collective-permute-start.10 = (bf16[2,32,512]{2,1,0:T(8,128)(2,1)S(1)}, bf16[2,32,512]{2,1,0:T(8,128)(2,1)S(1)}, u32[]{:S(2)}, u32[]{:S(2)}) collective-permute-start(bf16[2,32,512]{2,1,0:T(8,128)(2,1)S(1)} %get-tuple-element.46), channel_id=1, source_target_pairs={{0,8},{4,12},{8,0},{12,4},{16,24},{20,28},{24,16},{28,20},{1,9},{5... | collective-permute-start | bytes 196616 | tf_op jit(solution)/shard_map/ppermute | solution.py:332
  18.6 9.4 %collective-permute-start.11 = (bf16[2,32,512]{2,1,0:T(8,128)(2,1)S(1)}, bf16[2,32,512]{2,1,0:T(8,128)(2,1)S(1)}, u32[]{:S(2)}, u32[]{:S(2)}) collective-permute-start(bf16[2,32,512]{2,1,0:T(8,128)(2,1)S(1)} %get-tuple-element.47), channel_id=1, source_target_pairs={{0,12},{4,8},{8,4},{12,0},{16,28},{20,24},{24,20},{28,16},{1,13},{... | collective-permute-start | bytes 196616 | tf_op jit(solution)/shard_map/ppermute | solution.py:332
  19.9 9.0 %collective-permute-start.12 = (bf16[2,32,512]{2,1,0:T(8,128)(2,1)S(1)}, bf16[2,32,512]{2,1,0:T(8,128)(2,1)S(1)}, u32[]{:S(2)}, u32[]{:S(2)}) collective-permute-start(bf16[2,32,512]{2,1,0:T(8,128)(2,1)S(1)} %get-tuple-element.48), channel_id=1, source_target_pairs={{0,4},{4,0},{8,12},{12,8},{16,20},{20,16},{24,28},{28,24},{1,5},{5... | collective-permute-start | bytes 196616 | tf_op jit(solution)/shard_map/ppermute | solution.py:332
  20.5 8.5 %collective-permute-start.6 = (bf16[2,32,512]{2,1,0:T(8,128)(2,1)S(1)}, bf16[2,32,512]{2,1,0:T(8,128)(2,1)S(1)}, u32[]{:S(2)}, u32[]{:S(2)}) collective-permute-start(bf16[2,32,512]{2,1,0:T(8,128)(2,1)S(1)} %get-tuple-element.42), channel_id=1, source_target_pairs={{0,16},{4,20},{8,24},{12,28},{16,0},{20,4},{24,8},{28,12},{1,17},{... | collective-permute-start | bytes 196616 | tf_op jit(solution)/shard_map/ppermute | solution.py:332
  23.1 10.1 %collective-permute-start.7 = (bf16[2,32,512]{2,1,0:T(8,128)(2,1)S(1)}, bf16[2,32,512]{2,1,0:T(8,128)(2,1)S(1)}, u32[]{:S(2)}, u32[]{:S(2)}) collective-permute-start(bf16[2,32,512]{2,1,0:T(8,128)(2,1)S(1)} %get-tuple-element.43), channel_id=1, source_target_pairs={{0,20},{4,16},{8,28},{12,24},{16,4},{20,0},{24,12},{28,8},{1,21},{... | collective-permute-start | bytes 196616 | tf_op jit(solution)/shard_map/ppermute | solution.py:332
  24.3 8.8 %collective-permute-start.8 = (bf16[2,32,512]{2,1,0:T(8,128)(2,1)S(1)}, bf16[2,32,512]{2,1,0:T(8,128)(2,1)S(1)}, u32[]{:S(2)}, u32[]{:S(2)}) collective-permute-start(bf16[2,32,512]{2,1,0:T(8,128)(2,1)S(1)} %get-tuple-element.44), channel_id=1, source_target_pairs={{0,24},{4,28},{8,16},{12,20},{16,8},{20,12},{24,0},{28,4},{1,25},{... | collective-permute-start | bytes 196616 | tf_op jit(solution)/shard_map/ppermute | solution.py:332
  27.9 7.1 %collective-permute-start.9 = (bf16[2,32,512]{2,1,0:T(8,128)(2,1)S(1)}, bf16[2,32,512]{2,1,0:T(8,128)(2,1)S(1)}, u32[]{:S(2)}, u32[]{:S(2)}) collective-permute-start(bf16[2,32,512]{2,1,0:T(8,128)(2,1)S(1)} %get-tuple-element.45), channel_id=1, source_target_pairs={{0,28},{4,24},{8,20},{12,16},{16,12},{20,8},{24,4},{28,0},{1,29},{... | collective-permute-start | bytes 196616 | tf_op jit(solution)/shard_map/ppermute | solution.py:332
  28.2 0.7 %copy-start = (s32[8,8]{1,0:T(8,128)S(1)}, s32[8,8]{1,0:T(8,128)}, u32[]{:S(2)}) copy-start(s32[8,8]{1,0:T(8,128)} %refs_2_.1) | copy-start | bytes 772
  28.3 0.7 %copy-start.1 = (s32[8]{0:T(128)S(1)}, s32[8]{0:T(128)}, u32[]{:S(2)}) copy-start(s32[8]{0:T(128)} %param.11) | copy-start | bytes 100
  28.3 0.7 %copy-start.2 = (f32[16]{0:T(128)S(1)}, f32[16]{0:T(128)}, u32[]{:S(2)}) copy-start(f32[16]{0:T(128)} %param.13) | copy-start | bytes 196
  36.3 10.8 %collective-permute-start.17 = (bf16[2,32,512]{2,1,0:T(8,128)(2,1)S(1)}, bf16[2,32,512]{2,1,0:T(8,128)(2,1)S(1)}, u32[]{:S(2)}, u32[]{:S(2)}) collective-permute-start(bf16[2,32,512]{2,1,0:T(8,128)(2,1)S(1)} %get-tuple-element.53), channel_id=1, source_target_pairs={{0,8},{4,12},{8,0},{12,4},{16,24},{20,28},{24,16},{28,20},{1,9},{5... | collective-permute-start | bytes 196616 | tf_op jit(solution)/shard_map/ppermute | solution.py:332
  38.4 12.6 %collective-permute-start.18 = (bf16[2,32,512]{2,1,0:T(8,128)(2,1)S(1)}, bf16[2,32,512]{2,1,0:T(8,128)(2,1)S(1)}, u32[]{:S(2)}, u32[]{:S(2)}) collective-permute-start(bf16[2,32,512]{2,1,0:T(8,128)(2,1)S(1)} %get-tuple-element.54), channel_id=1, source_target_pairs={{0,12},{4,8},{8,4},{12,0},{16,28},{20,24},{24,20},{28,16},{1,13},{... | collective-permute-start | bytes 196616 | tf_op jit(solution)/shard_map/ppermute | solution.py:332
  38.9 14.1 %collective-permute-start.19 = (bf16[2,32,512]{2,1,0:T(8,128)(2,1)S(1)}, bf16[2,32,512]{2,1,0:T(8,128)(2,1)S(1)}, u32[]{:S(2)}, u32[]{:S(2)}) collective-permute-start(bf16[2,32,512]{2,1,0:T(8,128)(2,1)S(1)} %get-tuple-element.55), channel_id=1, source_target_pairs={{0,4},{4,0},{8,12},{12,8},{16,20},{20,16},{24,28},{28,24},{1,5},{5... | collective-permute-start | bytes 196616 | tf_op jit(solution)/shard_map/ppermute | solution.py:332
  41.7 11.3 %collective-permute-start.14 = (bf16[2,32,512]{2,1,0:T(8,128)(2,1)S(1)}, bf16[2,32,512]{2,1,0:T(8,128)(2,1)S(1)}, u32[]{:S(2)}, u32[]{:S(2)}) collective-permute-start(bf16[2,32,512]{2,1,0:T(8,128)(2,1)S(1)} %get-tuple-element.50), channel_id=1, source_target_pairs={{0,20},{4,16},{8,28},{12,24},{16,4},{20,0},{24,12},{28,8},{1,21},{... | collective-permute-start | bytes 196616 | tf_op jit(solution)/shard_map/ppermute | solution.py:332
  45.3 7.7 %collective-permute-start.15 = (bf16[2,32,512]{2,1,0:T(8,128)(2,1)S(1)}, bf16[2,32,512]{2,1,0:T(8,128)(2,1)S(1)}, u32[]{:S(2)}, u32[]{:S(2)}) collective-permute-start(bf16[2,32,512]{2,1,0:T(8,128)(2,1)S(1)} %get-tuple-element.51), channel_id=1, source_target_pairs={{0,24},{4,28},{8,16},{12,20},{16,8},{20,12},{24,0},{28,4},{1,25},{... | collective-permute-start | bytes 196616 | tf_op jit(solution)/shard_map/ppermute | solution.py:332
  47.2 7.1 %collective-permute-start.16 = (bf16[2,32,512]{2,1,0:T(8,128)(2,1)S(1)}, bf16[2,32,512]{2,1,0:T(8,128)(2,1)S(1)}, u32[]{:S(2)}, u32[]{:S(2)}) collective-permute-start(bf16[2,32,512]{2,1,0:T(8,128)(2,1)S(1)} %get-tuple-element.52), channel_id=1, source_target_pairs={{0,28},{4,24},{8,20},{12,16},{16,12},{20,8},{24,4},{28,0},{1,29},{... | collective-permute-start | bytes 196616 | tf_op jit(solution)/shard_map/ppermute | solution.py:332
  51.0 5.5 %collective-permute-start.13 = (bf16[2,32,512]{2,1,0:T(8,128)(2,1)S(1)}, bf16[2,32,512]{2,1,0:T(8,128)(2,1)S(1)}, u32[]{:S(2)}, u32[]{:S(2)}) collective-permute-start(bf16[2,32,512]{2,1,0:T(8,128)(2,1)S(1)} %energy.4), channel_id=1, source_target_pairs={{0,16},{4,20},{8,24},{12,28},{16,0},{20,4},{24,8},{28,12},{1,17},{... | collective-permute-start | bytes 196616 | tf_op jit(solution)/shard_map/ppermute | solution.py:332
